TPU v7x, 32 devices: a whole 2x2x4 slice. The times are simulated.
32 devices in a mesh: row: 4 (over z), leaf: 8 (over y, x, core).
Axes of the slice: x: 2, y: 2, z: 4, core: 2. Of those that a mesh axis runs over, the one named last changes fastest.
Arguments:
- leaf_update: float32 [16384, 256], P(('leaf', 'row')), may hold values from -6 to 6
- rhs: float32 [3, 16384, 256], P(None, ('leaf', 'row')), may hold values from -6 to 6
- inv_top: bfloat16 [2, 16384, 8, 4, 512], P(None, 'leaf', None, 'row'), may hold values from -0.03125 to 0.03125
- inv_mid: bfloat16 [2, 16384, 4, 4, 512], P(None, 'leaf', None, 'row'), may hold values from -0.046875 to 0.046875
- inv_low: bfloat16 [2, 16384, 2, 4, 512], P(None, 'leaf', None, 'row'), may hold values from -0.0625 to 0.0625
- couple_mid: bfloat16 [2, 16384, 4, 4, 512], P(None, 'leaf', None, 'row'), may hold values from -0.046875 to 0.046875
- couple_low: bfloat16 [2, 16384, 2, 4, 512], P(None, 'leaf', None, 'row'), may hold values from -0.0625 to 0.0625
- block_map: int32 [3, 128], P(None, ('leaf', 'row')), may hold values from 0 to 127, as said below
Outputs:
- solution: float32 [3, 16384, 256], P(None, ('leaf', 'row'))
- leaf_solution: float32 [16384, 256], P(('leaf', 'row'))
Inputs may be any that keep to these rules, and one draw needn't show every extreme that they name: Device d of the group of a front holds rows d * 512 to (d + 1) * 512 - 1 of the front's separator part and the same rows of its update part, with d = p * 4 + r for group position p (leaf index modulo the group size) and row index r. block_map[k] is one to one within each parent, and a block held at row index r and group position p of a child lands on a parent block held at row index r and group position p or p + (group size of the parent) / 2. At level 0 every parent block receives one block.
All inputs are finite; a program needn't handle non-finite values.
Results may differ from a plain program's by a relative error of at most 0.012.
Values may be sent and summed in bfloat16 or wider, within the bound.
A program may use at most 256 MiB of HBM per device.

v0:
```python
import jax
import jax.numpy as jnp
from jax import lax
from jax.sharding import PartitionSpec as P

BLOCK = 128


def partner_2(block, axis, distance):
    count = lax.axis_size(axis)
    route = []
    for low in range(count):
        high = low | 1 << distance
        if high != low and high < count:
            route += [(low, high), (high, low)]
    return lax.ppermute(block, axis, route)


def complex_apply(real_part, imag_part, right_side, transpose):
    half_cols = right_side.shape[1] // 2
    if transpose:
        dim_numbers = (((0,), (0,)), ((), ()))
    else:
        dim_numbers = (((1,), (0,)), ((), ()))
    product_real = lax.dot_general(
        real_part, right_side, dim_numbers, preferred_element_type=jnp.float32
    )
    product_imag = lax.dot_general(
        imag_part, right_side, dim_numbers, preferred_element_type=jnp.float32
    )
    return jnp.concatenate(
        [
            product_real[:, :half_cols] - product_imag[:, half_cols:],
            product_real[:, half_cols:] + product_imag[:, :half_cols],
        ],
        axis=1,
    )


def panel_parts(panel_tile):
    merged = panel_tile.reshape(
        2, panel_tile.shape[1], panel_tile.shape[2] * panel_tile.shape[3] * panel_tile.shape[4]
    )
    return (merged[0], merged[1])


def subgroup_gather(vector, bit_count, leaf_pos):
    gathered = vector
    for bit_pos in range(bit_count):
        partner = partner_2(gathered, "leaf", bit_pos)
        upper_half = leaf_pos >> bit_pos & 1 == 1
        gathered = jnp.where(
            upper_half,
            jnp.concatenate([partner, gathered], axis=0),
            jnp.concatenate([gathered, partner], axis=0),
        )
    return gathered


def subgroup_sum(partial_value, bit_count, leaf_pos, slice_rows):
    total_sum = partial_value
    for bit_pos in range(bit_count):
        total_sum = total_sum + partner_2(total_sum, "leaf", bit_pos)
    position = leaf_pos & (1 << bit_count) - 1
    return lax.dynamic_slice_in_dim(total_sum, position * slice_rows, slice_rows, 0)


def row_reduced(panel_tile, gathered):
    real_part, imag_part = panel_parts(panel_tile)
    return lax.psum_scatter(
        complex_apply(real_part, imag_part, gathered, False), "row", scatter_dimension=0, tiled=True
    )


def row_folded(panel_tile, vector_half):
    real_part, imag_part = panel_parts(panel_tile)
    return complex_apply(
        real_part, imag_part, lax.all_gather(vector_half, "row", axis=0, tiled=True), True
    )


def slot_ids(position, row_pos, row_size, blocks_dev, sep_blocks, has_update):
    own_slots = (position * row_size + row_pos) * blocks_dev + jnp.arange(
        blocks_dev, dtype=jnp.int32
    )
    if has_update:
        return jnp.concatenate([own_slots, own_slots + sep_blocks])
    return own_slots


def extend_add(child_rows, targets, rhs_part, bit_count, has_update, leaf_pos, row_pos, row_size):
    bit_pos = bit_count - 1
    partner_rows, partner_targets = partner_2((child_rows, targets), "leaf", bit_pos)
    blocks_dev = targets.shape[0]
    group_size = 1 << bit_count
    position = leaf_pos & group_size - 1
    sep_blocks = group_size * row_size * blocks_dev
    slot_list = slot_ids(position, row_pos, row_size, blocks_dev, sep_blocks, has_update)
    candidates = jnp.concatenate([targets, partner_targets])
    columns = child_rows.shape[1]
    block_pool = jnp.concatenate([child_rows, partner_rows], axis=0).reshape(2 * blocks_dev, -1)
    selector = (slot_list[:, None] == candidates[None, :]).astype(jnp.float32)
    placed = jnp.dot(
        selector, block_pool, precision=lax.Precision.HIGHEST, preferred_element_type=jnp.float32
    ).reshape(-1, columns)
    slice_rows = rhs_part.shape[0]
    return (placed[:slice_rows] + rhs_part, placed[slice_rows:])


def extend_down(front_rows, targets, bit_count, leaf_pos, row_pos, row_size):
    bit_pos = bit_count - 1
    partner_rows = partner_2(front_rows, "leaf", bit_pos)
    blocks_dev = targets.shape[0]
    has_update = front_rows.shape[0] > blocks_dev * BLOCK
    group_size = 1 << bit_count
    position = leaf_pos & group_size - 1
    sep_blocks = group_size * row_size * blocks_dev
    own_slots = slot_ids(position, row_pos, row_size, blocks_dev, sep_blocks, has_update)
    partner_slots = slot_ids(
        position ^ group_size // 2, row_pos, row_size, blocks_dev, sep_blocks, has_update
    )
    columns = front_rows.shape[1]
    block_pool = jnp.concatenate([front_rows, partner_rows], axis=0).reshape(-1, BLOCK * columns)
    selector = (targets[:, None] == jnp.concatenate([own_slots, partner_slots])[None, :]).astype(
        jnp.float32
    )
    return jnp.dot(
        selector, block_pool, precision=lax.Precision.HIGHEST, preferred_element_type=jnp.float32
    ).reshape(-1, columns)


def shards(leaf_update, rhs, inv_top, inv_mid, inv_low, couple_mid, couple_low, block_map):
    leaf_pos = lax.axis_index("leaf")
    row_pos = lax.axis_index("row")
    row_size = lax.axis_size("row")
    leaf_bits = lax.axis_size("leaf").bit_length() - 1
    slice_rows = rhs.shape[1]
    inverses = (inv_top, inv_mid, inv_low)
    couplings = (None, couple_mid, couple_low)
    children = leaf_update
    saved_y = [None, None, None]
    for level_index in (2, 1):
        bit_count = leaf_bits - level_index
        sep_part, update_part = extend_add(
            children,
            block_map[level_index],
            rhs[level_index],
            bit_count,
            True,
            leaf_pos,
            row_pos,
            row_size,
        )
        gathered = subgroup_gather(sep_part.astype(jnp.bfloat16), bit_count, leaf_pos)
        solved = row_reduced(inverses[level_index], gathered)
        saved_y[level_index] = solved
        gathered_y = subgroup_gather(solved.astype(jnp.bfloat16), bit_count, leaf_pos)
        children = update_part - row_reduced(couplings[level_index], gathered_y)
    sep_top, unused_rows = extend_add(
        children, block_map[0], rhs[0], leaf_bits, False, leaf_pos, row_pos, row_size
    )
    gathered = lax.all_gather(sep_top.astype(jnp.bfloat16), "leaf", axis=0, tiled=True)
    y_top = row_reduced(inv_top, gathered)
    partial_value = row_folded(inv_top, y_top.astype(jnp.bfloat16))
    x_top = lax.psum_scatter(partial_value, "leaf", scatter_dimension=0, tiled=True)
    solutions = [x_top]
    front_rows = x_top
    for level_index in (1, 2):
        bit_count = leaf_bits - level_index
        x_update = extend_down(
            front_rows, block_map[level_index - 1], bit_count + 1, leaf_pos, row_pos, row_size
        )
        coupled = subgroup_sum(
            row_folded(couplings[level_index], x_update.astype(jnp.bfloat16)),
            bit_count,
            leaf_pos,
            slice_rows,
        )
        reduced = saved_y[level_index] - coupled
        x_sep = subgroup_sum(
            row_folded(inverses[level_index], reduced.astype(jnp.bfloat16)),
            bit_count,
            leaf_pos,
            slice_rows,
        )
        solutions.append(x_sep)
        front_rows = jnp.concatenate([x_sep, x_update], axis=0)
    leaf_solution = extend_down(
        front_rows, block_map[2], leaf_bits - 2, leaf_pos, row_pos, row_size
    )
    return (jnp.stack(solutions), leaf_solution)


def solution(mesh):
    return jax.shard_map(
        shards,
        mesh=mesh,
        in_specs=(
            P(("leaf", "row"), None),
            P(None, ("leaf", "row"), None),
            P(None, "leaf", None, "row", None),
            P(None, "leaf", None, "row", None),
            P(None, "leaf", None, "row", None),
            P(None, "leaf", None, "row", None),
            P(None, "leaf", None, "row", None),
            P(None, ("leaf", "row")),
        ),
        out_specs=(P(None, ("leaf", "row"), None), P(("leaf", "row"), None)),
        check_vma=False,
    )
```

profile of v0, /device:TPU:0, one launch (start us, length us, event | category | flops | bytes accessed | tf_op | source)
XLA Modules:
  0.0 893.9 jit_solution(10732206832914136317)
XLA Ops:
  13.0 8.4 fusion.49
  21.4 3.5 copy.38
  31.8 45.7 %reduce-scatter.7.cloned.1.call-done = f32[512,256]{0,1:T(8,128)} async-done(((f32[2048,256]{0,1:T(8,128)}), f32[512,256]{0,1:T(8,128)}) %reduce-scatter.7.cloned.1.call-update) | async-done | bytes 524304 | tf_op jit(solution)/shard_map/reduce_scatter | solution.py:70
  78.6 7.1 fusion.48
  94.0 42.5 %reduce-scatter.9.cloned.1.call-done = f32[512,256]{0,1:T(8,128)} async-done(((f32[2048,256]{0,1:T(8,128)}), f32[512,256]{0,1:T(8,128)}) %reduce-scatter.9.cloned.1.call-update) | async-done | bytes 524304 | tf_op jit(solution)/shard_map/reduce_scatter | solution.py:70
  140.1 11.0 %collective-permute-done.1 = s32[4]{0:T(128)S(1)} collective-permute-done((s32[4]{0:T(128)S(1)}, s32[4]{0:T(128)S(1)}, u32[]{:S(2)}, u32[]{:S(2)}) %collective-permute-start.1) | collective-permute-done | bytes 48 | tf_op jit(solution)/shard_map/ppermute | solution.py:16
  155.0 1.6 collective-permute-start.8
  156.6 15.9 %fusion.47 = (bf16[1,2048,4,1,512]{4,2,3,1,0:T(4,128)(2,1)}, bf16[1,2048,4,1,512]{4,2,3,1,0:T(4,128)(2,1)}) fusion(bf16[2,2048,4,1,512]{4,2,3,1,0:T(4,128)(2,1)} %param.11), kind=kLoop, calls=%fused_computation.142 | loop fusion | bytes 33554432 | tf_op jit(solution)/shard_map/slice | solution.py:44
  172.4 10.3 %copy.42 = bf16[256,8,4,512]{3,1,2,0:T(8,128)(2,1)} copy(bf16[256,8,4,512]{3,2,1,0:T(4,128)(2,1)} %bitcast.146) | data formatting | bytes 16777216
  182.8 10.3 %copy.43 = bf16[256,8,4,512]{3,1,2,0:T(8,128)(2,1)} copy(bf16[256,8,4,512]{3,2,1,0:T(4,128)(2,1)} %bitcast.145) | data formatting | bytes 16777216
  193.1 5.9 convolution_bitcast_fusion.10
  199.0 2.4 convolution_bitcast_fusion.11
  203.6 42.4 %reduce-scatter.11.cloned.1.call-done = f32[512,256]{0,1:T(8,128)} async-done(((f32[2048,256]{0,1:T(8,128)}), f32[512,256]{0,1:T(8,128)}) %reduce-scatter.11.cloned.1.call-update) | async-done | bytes 524304 | tf_op jit(solution)/shard_map/reduce_scatter | solution.py:70
  248.8 1.5 collective-permute-start.10
  250.3 15.7 %fusion.46 = (bf16[1,2048,4,1,512]{4,2,3,1,0:T(4,128)(2,1)}, bf16[1,2048,4,1,512]{4,2,3,1,0:T(4,128)(2,1)}) fusion(bf16[2,2048,4,1,512]{4,2,3,1,0:T(4,128)(2,1)} %param.13), kind=kLoop, calls=%fused_computation.141 | loop fusion | bytes 33554432 | tf_op jit(solution)/shard_map/slice | solution.py:44
  266.1 10.3 %copy.44 = bf16[256,8,4,512]{3,1,2,0:T(8,128)(2,1)} copy(bf16[256,8,4,512]{3,2,1,0:T(4,128)(2,1)} %bitcast.148) | data formatting | bytes 16777216
  276.4 10.3 %copy.45 = bf16[256,8,4,512]{3,1,2,0:T(8,128)(2,1)} copy(bf16[256,8,4,512]{3,2,1,0:T(4,128)(2,1)} %bitcast.147) | data formatting | bytes 16777216
  286.6 5.9 convolution_bitcast_fusion.8
  292.6 2.4 convolution_bitcast_fusion.9
  297.5 41.5 %reduce-scatter.13.cloned.1.call-done = f32[512,256]{0,1:T(8,128)} async-done(((f32[2048,256]{0,1:T(8,128)}), f32[512,256]{0,1:T(8,128)}) %reduce-scatter.13.cloned.1.call-update) | async-done | bytes 524304 | tf_op jit(solution)/shard_map/reduce_scatter | solution.py:70
  340.0 1.5 collective-permute-start.11
  342.1 11.3 %collective-permute-done = s32[4]{0:T(128)S(1)} collective-permute-done((s32[4]{0:T(128)S(1)}, s32[4]{0:T(128)S(1)}, u32[]{:S(2)}, u32[]{:S(2)}) %collective-permute-start) | collective-permute-done | bytes 48 | tf_op jit(solution)/shard_map/ppermute | solution.py:16
  355.2 1.8 fusion.8
  357.1 12.1 %fusion.45 = (bf16[1,2048,8,1,512]{4,2,3,1,0:T(8,128)(2,1)S(1)}, bf16[1,2048,8,1,512]{4,2,3,1,0:T(8,128)(2,1)S(1)}) fusion(bf16[2,2048,8,1,512]{4,2,3,1,0:T(8,128)(2,1)} %param.10), kind=kLoop, calls=%fused_computation.140 | loop fusion | bytes 67108864 | tf_op jit(solution)/shard_map/slice | solution.py:44
  369.2 10.8 %copy.46 = bf16[256,8,8,512]{3,1,2,0:T(8,128)(2,1)} copy(bf16[256,8,8,512]{3,2,1,0:T(8,128)(2,1)S(1)} %bitcast.140) | data formatting | bytes 33554432
  380.0 10.7 %copy.47 = bf16[256,8,8,512]{3,1,2,0:T(8,128)(2,1)} copy(bf16[256,8,8,512]{3,2,1,0:T(8,128)(2,1)S(1)} %bitcast.139) | data formatting | bytes 33554432
  390.7 8.8 convolution_bitcast_fusion.6
  399.5 12.4 %convolution_bitcast_fusion.7 = f32[2048,256]{0,1:T(8,128)} fusion(bf16[4096,256]{1,0:T(8,128)(2,1)} %all-gather.7.cloned.1.call-done, bf16[2048,4096]{1,0:T(8,128)(2,1)} %bitcast.149), kind=kOutput, calls=%fused_computation.8 | convolution fusion | flops 4294967296 | bytes 20971520 | tf_op jit(solution)/shard_map/dot_general | solution.py:25
  411.9 1.8 slice_subtract_fusion.3
  415.2 43.2 %reduce-scatter.15.cloned.1.call-done = f32[512,256]{0,1:T(8,128)} async-done(((f32[2048,256]{0,1:T(8,128)}), f32[512,256]{0,1:T(8,128)}) %reduce-scatter.15.cloned.1.call-update) | async-done | bytes 524304 | tf_op jit(solution)/shard_map/reduce_scatter | solution.py:70
  458.4 1.8 convert_element_type.41
  460.3 27.5 %all-gather.9.cloned.1.call-done = bf16[2048,256]{0,1:T(8,128)(2,1)} async-done(((bf16[512,256]{0,1:T(8,128)(2,1)}), bf16[2048,256]{0,1:T(8,128)(2,1)}) %all-gather.9.cloned.1.call-update) | async-done | bytes 1048592 | tf_op jit(solution)/shard_map/all_gather | solution.py:78
  487.8 10.6 %convolution_bitcast_fusion = f32[4096,256]{0,1:T(8,128)S(1)} fusion(bf16[2048,256]{0,1:T(8,128)(2,1)} %all-gather.9.cloned.1.call-done, bf16[2048,4096]{1,0:T(8,128)(2,1)} %bitcast.152), kind=kOutput, calls=%fused_computation | convolution fusion | flops 4294967296 | bytes 22020096 | tf_op jit(solution)/shard_map/dot_general | solution.py:28
  498.5 8.2 convolution_bitcast_fusion.1
  507.3 2.3 pad_maximum_fusion
  509.7 50.6 %reduce-scatter.17.cloned.1.call-done = f32[512,256]{0,1:T(8,128)} async-done(((f32[4096,256]{0,1:T(8,128)}), f32[512,256]{0,1:T(8,128)}) %reduce-scatter.17.cloned.1.call-update) | async-done | bytes 524304 | tf_op jit(solution)/shard_map/reduce_scatter | solution.py:165
  561.8 12.2 %collective-permute-done.12 = f32[512,256]{0,1:T(8,128)S(1)} collective-permute-done((f32[512,256]{0,1:T(8,128)}, f32[512,256]{0,1:T(8,128)S(1)}, u32[]{:S(2)}, u32[]{:S(2)}) %collective-permute-start.12) | collective-permute-done | bytes 524320 | tf_op jit(solution)/shard_map/ppermute | solution.py:16
  577.5 28.1 %all-gather.11.cloned.1.call-done = bf16[2048,256]{1,0:T(8,128)(2,1)} async-done(((bf16[512,256]{1,0:T(8,128)(2,1)}), bf16[2048,256]{1,0:T(8,128)(2,1)}) %all-gather.11.cloned.1.call-update) | async-done | bytes 1048592 | tf_op jit(solution)/shard_map/all_gather | solution.py:78
  605.5 6.1 convolution_bitcast_fusion.4
  611.7 5.7 convolution_bitcast_fusion.5
  618.0 4.1 collective-permute-done.13
  622.4 1.5 collective-permute-start.14
  623.9 46.3 %collective-permute-done.14 = f32[2048,256]{0,1:T(8,128)} collective-permute-done((f32[2048,256]{0,1:T(8,128)S(1)}, f32[2048,256]{0,1:T(8,128)}, u32[]{:S(2)}, u32[]{:S(2)}) %collective-permute-start.14) | collective-permute-done | bytes 2097184 | tf_op jit(solution)/shard_map/ppermute | solution.py:16
  670.3 1.9 fusion.7
  672.6 27.1 %all-gather.13.cloned.1.call-done = bf16[2048,256]{0,1:T(8,128)(2,1)} async-done(((bf16[512,256]{0,1:T(8,128)(2,1)}), bf16[2048,256]{0,1:T(8,128)(2,1)}) %all-gather.13.cloned.1.call-update) | async-done | bytes 1048592 | tf_op jit(solution)/shard_map/all_gather | solution.py:78
  699.7 6.1 convolution_bitcast_fusion.2
  705.8 5.7 convolution_bitcast_fusion.3
  712.1 4.1 collective-permute-done.15
  716.3 1.6 fusion.43
  719.6 46.3 %collective-permute-done.16 = f32[2048,256]{0,1:T(8,128)} collective-permute-done((f32[2048,256]{0,1:T(8,128)}, f32[2048,256]{0,1:T(8,128)}, u32[]{:S(2)}, u32[]{:S(2)}) %collective-permute-start.16) | collective-permute-done | bytes 2097184 | tf_op jit(solution)/shard_map/ppermute | solution.py:16
  767.2 1.5 collective-permute-start.17
  768.9 22.8 %collective-permute-done.17 = f32[1024,256]{0,1:T(8,128)} collective-permute-done((f32[1024,256]{0,1:T(8,128)S(1)}, f32[1024,256]{0,1:T(8,128)}, u32[]{:S(2)}, u32[]{:S(2)}) %collective-permute-start.17) | collective-permute-done | bytes 1048608 | tf_op jit(solution)/shard_map/ppermute | solution.py:16
  793.1 1.8 copy.31
  795.0 1.7 reshape.91
  798.9 27.3 %all-gather.15.cloned.1.call-done = bf16[2048,256]{1,0:T(8,128)(2,1)} async-done(((bf16[512,256]{1,0:T(8,128)(2,1)}), bf16[2048,256]{1,0:T(8,128)(2,1)}) %all-gather.15.cloned.1.call-update) | async-done | bytes 1048592 | tf_op jit(solution)/shard_map/all_gather | solution.py:78
  826.2 3.9 convolution_bitcast_fusion.18
  832.7 3.0 collective-permute-done.18
  835.7 1.9 fusion.5
  837.6 27.5 %all-gather.17.cloned.1.call-done = bf16[2048,256]{0,1:T(8,128)(2,1)} async-done(((bf16[512,256]{0,1:T(8,128)(2,1)}), bf16[2048,256]{0,1:T(8,128)(2,1)}) %all-gather.17.cloned.1.call-update) | async-done | bytes 1048592 | tf_op jit(solution)/shard_map/all_gather | solution.py:78
  865.2 3.9 convolution_bitcast_fusion.16
  871.9 2.8 collective-permute-done.19
  877.2 1.6 copy.35
  881.3 1.8 copy.34
  883.1 1.7 reshape.93
  (215 shorter events, 68.1 us)
Async XLA Ops:
  7.2 3.5 copy-start.15
  7.2 70.3 %reduce-scatter.7.cloned.1.call-start = ((), (), s32[]{:S(2)}) async-start(), calls=%async_computation.6 | async-start | bytes 2621440 | tf_op jit(solution)/shard_map/reduce_scatter | solution.py:70
  8.0 2.3 copy-start.16
  8.0 143.0 %copy-start.18 = (s32[4]{0:T(128)}, s32[4]{0:T(128)S(1)}, u32[]{:S(2)}) copy-start(s32[4]{0:T(128)S(1)} %get-tuple-element.44) | copy-start | bytes 52
  8.0 2.2 collective-permute-start.2
  8.6 2.1 collective-permute-start.3
  10.1 0.5 copy-start.20
  12.5 13.7 %collective-permute-start.4 = (bf16[512,256]{0,1:T(8,128)(2,1)S(1)}, bf16[512,256]{0,1:T(8,128)(2,1)S(1)}, u32[]{:S(2)}, u32[]{:S(2)}) collective-permute-start(bf16[512,256]{0,1:T(8,128)(2,1)S(1)} %fusion.10), channel_id=1, source_target_pairs={{0,1},{1,0},{2,3},{3,2},{4,5},{5,4},{6,7},{7,6},{8,9},{9,8},{10,11... | collective-permute-start | bytes 786440 | tf_op jit(solution)/shard_map/ppermute | solution.py:16
  21.4 3.5 copy-start.1
  24.9 3.4 copy-start.6
  26.1 2.1 copy-start.8
  31.3 105.2 %reduce-scatter.9.cloned.1.call-start = ((), (), s32[]{:S(2)}) async-start(), calls=%async_computation.7 | async-start | bytes 2621440 | tf_op jit(solution)/shard_map/reduce_scatter | solution.py:70
  78.6 9.6 %collective-permute-start.5 = (bf16[512,256]{0,1:T(8,128)(2,1)S(1)}, bf16[512,256]{0,1:T(8,128)(2,1)S(1)}, u32[]{:S(2)}, u32[]{:S(2)}) collective-permute-start(bf16[512,256]{0,1:T(8,128)(2,1)S(1)} %convert_element_type.37), channel_id=1, source_target_pairs={{0,1},{1,0},{2,3},{3,2},{4,5},{5,4},{6,7},{7,6},{8,9},{9,8},{10,11... | collective-permute-start | bytes 786440 | tf_op jit(solution)/shard_map/ppermute | solution.py:16
  87.0 3.4 copy-start.9
  88.2 2.2 copy-start.11
  93.4 152.6 %reduce-scatter.11.cloned.1.call-start = ((), (), s32[]{:S(2)}) async-start(), calls=%async_computation.8 | async-start | bytes 2621440 | tf_op jit(solution)/shard_map/reduce_scatter | solution.py:70
  137.6 13.5 %collective-permute-start.6 = (f32[512,256]{0,1:T(8,128)S(1)}, f32[512,256]{0,1:T(8,128)S(1)}, u32[]{:S(2)}, u32[]{:S(2)}) collective-permute-start(f32[512,256]{0,1:T(8,128)S(1)} %sub.44), channel_id=1, source_target_pairs={{0,2},{2,0},{1,3},{3,1},{4,6},{6,4},{5,7},{7,5},{8,10},{10,8},{9,1... | collective-permute-start | bytes 1572872 | tf_op jit(solution)/shard_map/ppermute | solution.py:16
  139.1 11.9 %collective-permute-start.1 = (s32[4]{0:T(128)S(1)}, s32[4]{0:T(128)S(1)}, u32[]{:S(2)}, u32[]{:S(2)}) collective-permute-start(s32[4]{0:T(128)S(1)} %get-tuple-element.44), channel_id=1, source_target_pairs={{0,2},{2,0},{1,3},{3,1},{4,6},{6,4},{5,7},{7,5},{8,10},{10,8},{9,1... | collective-permute-start | bytes 56 | tf_op jit(solution)/shard_map/ppermute | solution.py:16
  139.9 11.6 %copy-start.24 = (s32[4]{0:T(128)}, s32[4]{0:T(128)S(1)}, u32[]{:S(2)}) copy-start(s32[4]{0:T(128)S(1)} %broadcast_add_fusion.3) | copy-start | bytes 52
  140.0 11.6 %copy-start.26 = (s32[4]{0:T(128)}, s32[4]{0:T(128)S(1)}, u32[]{:S(2)}) copy-start(s32[4]{0:T(128)S(1)} %iota_add_fusion.4) | copy-start | bytes 52
  153.3 1.6 collective-permute-start.7
  155.0 38.1 %collective-permute-start.8 = (bf16[1024,256]{0,1:T(8,128)(2,1)S(1)}, bf16[1024,256]{0,1:T(8,128)(2,1)S(1)}, u32[]{:S(2)}, u32[]{:S(2)}) collective-permute-start(bf16[1024,256]{0,1:T(8,128)(2,1)S(1)} %maximum_select_fusion.4), channel_id=1, source_target_pairs={{0,2},{2,0},{1,3},{3,1},{4,6},{6,4},{5,7},{7,5},{8,10},{10,8},{9,1... | collective-permute-start | bytes 1572872 | tf_op jit(solution)/shard_map/ppermute | solution.py:16
  193.1 5.9 copy-start.3
  203.5 135.4 %reduce-scatter.13.cloned.1.call-start = ((), (), s32[]{:S(2)}) async-start(), calls=%async_computation.9 | async-start | bytes 2621440 | tf_op jit(solution)/shard_map/reduce_scatter | solution.py:70
  247.0 1.6 collective-permute-start.9
  248.8 37.8 %collective-permute-start.10 = (bf16[1024,256]{0,1:T(8,128)(2,1)S(1)}, bf16[1024,256]{0,1:T(8,128)(2,1)S(1)}, u32[]{:S(2)}, u32[]{:S(2)}) collective-permute-start(bf16[1024,256]{0,1:T(8,128)(2,1)S(1)} %maximum_select_fusion.5), channel_id=1, source_target_pairs={{0,2},{2,0},{1,3},{3,1},{4,6},{6,4},{5,7},{7,5},{8,10},{10,8},{9,1... | collective-permute-start | bytes 1572872 | tf_op jit(solution)/shard_map/ppermute | solution.py:16
  286.6 5.9 copy-start
  296.8 93.9 %all-gather.7.cloned.1.call-start = ((), (), s32[]{:S(2)}) async-start(), calls=%async_computation.10 | async-start | bytes 2359296 | tf_op jit(solution)/shard_map/all_gather | solution.py:162
  340.0 13.5 %collective-permute-start.11 = (f32[512,256]{0,1:T(8,128)S(1)}, f32[512,256]{0,1:T(8,128)S(1)}, u32[]{:S(2)}, u32[]{:S(2)}) collective-permute-start(f32[512,256]{0,1:T(8,128)S(1)} %sub.47), channel_id=1, source_target_pairs={{0,4},{4,0},{1,5},{5,1},{2,6},{6,2},{3,7},{7,3},{8,12},{12,8},{9,1... | collective-permute-start | bytes 1572872 | tf_op jit(solution)/shard_map/ppermute | solution.py:16
  341.6 11.9 %collective-permute-start = (s32[4]{0:T(128)S(1)}, s32[4]{0:T(128)S(1)}, u32[]{:S(2)}, u32[]{:S(2)}) collective-permute-start(s32[4]{0:T(128)S(1)} %get-tuple-element.42), channel_id=1, source_target_pairs={{0,4},{4,0},{1,5},{5,1},{2,6},{6,2},{3,7},{7,3},{8,12},{12,8},{9,1... | collective-permute-start | bytes 56 | tf_op jit(solution)/shard_map/ppermute | solution.py:16
  357.0 101.4 %reduce-scatter.15.cloned.1.call-start = ((), (), s32[]{:S(2)}) async-start(), calls=%async_computation.11 | async-start | bytes 2621440 | tf_op jit(solution)/shard_map/reduce_scatter | solution.py:70
  415.2 72.6 %all-gather.9.cloned.1.call-start = ((), (), s32[]{:S(2)}) async-start(), calls=%async_computation.12 | async-start | bytes 1310720 | tf_op jit(solution)/shard_map/all_gather | solution.py:78
  460.2 100.0 %reduce-scatter.17.cloned.1.call-start = ((), (), s32[]{:S(2)}) async-start(), calls=%async_computation.13 | async-start | bytes 4718592 | tf_op jit(solution)/shard_map/reduce_scatter | solution.py:165
  487.8 10.7 %copy-start.28 = (bf16[2048,256]{0,1:T(8,128)(2,1)S(1)}, bf16[2048,256]{0,1:T(8,128)(2,1)}, u32[]{:S(2)}) copy-start(bf16[2048,256]{0,1:T(8,128)(2,1)} %all-gather.9.cloned.1.call-done) | copy-start | bytes 3145732
  509.6 95.9 %all-gather.11.cloned.1.call-start = ((), (), s32[]{:S(2)}) async-start(), calls=%async_computation.14 | async-start | bytes 1310720 | tf_op jit(solution)/shard_map/all_gather | solution.py:78
  560.2 13.7 %collective-permute-start.12 = (f32[512,256]{0,1:T(8,128)}, f32[512,256]{0,1:T(8,128)S(1)}, u32[]{:S(2)}, u32[]{:S(2)}) collective-permute-start(f32[512,256]{0,1:T(8,128)} %reduce-scatter.17.cloned.1.call-done), channel_id=1, source_target_pairs={{0,4},{4,0},{1,5},{5,1},{2,6},{6,2},{3,7},{7,3},{8,12},{12,8},{9,1... | collective-permute-start | bytes 1572872 | tf_op jit(solution)/shard_map/ppermute | solution.py:16
  577.4 122.3 %all-gather.13.cloned.1.call-start = ((), (), s32[]{:S(2)}) async-start(), calls=%async_computation.15 | async-start | bytes 1310720 | tf_op jit(solution)/shard_map/all_gather | solution.py:78
  605.5 6.1 copy-start.2
  617.9 52.3 %copy-start.13 = (f32[512,256]{0,1:T(8,128)S(1)}, f32[512,256]{0,1:T(8,128)}, u32[]{:S(2)}) copy-start(f32[512,256]{0,1:T(8,128)} %reduce-scatter.11.cloned.1.call-done) | copy-start | bytes 1572868
  617.9 4.2 collective-permute-start.13
  622.4 47.8 %collective-permute-start.14 = (f32[2048,256]{0,1:T(8,128)S(1)}, f32[2048,256]{0,1:T(8,128)}, u32[]{:S(2)}, u32[]{:S(2)}) collective-permute-start(f32[2048,256]{0,1:T(8,128)S(1)} %fusion.44), channel_id=1, source_target_pairs={{0,2},{2,0},{1,3},{3,1},{4,6},{6,4},{5,7},{7,5},{8,10},{10,8},{9,1... | collective-permute-start | bytes 6291464 | tf_op jit(solution)/shard_map/ppermute | solution.py:16
  672.2 154.0 %all-gather.15.cloned.1.call-start = ((), (), s32[]{:S(2)}) async-start(), calls=%async_computation.16 | async-start | bytes 1310720 | tf_op jit(solution)/shard_map/all_gather | solution.py:78
  699.7 6.1 copy-start.29
  712.0 4.2 collective-permute-start.15
  717.9 48.0 %collective-permute-start.16 = (f32[2048,256]{0,1:T(8,128)}, f32[2048,256]{0,1:T(8,128)}, u32[]{:S(2)}, u32[]{:S(2)}) collective-permute-start(f32[2048,256]{0,1:T(8,128)} %fusion.43), channel_id=1, source_target_pairs={{0,2},{2,0},{1,3},{3,1},{4,6},{6,4},{5,7},{7,5},{8,10},{10,8},{9,1... | collective-permute-start | bytes 6291464 | tf_op jit(solution)/shard_map/ppermute | solution.py:16
  719.5 49.3 %copy-start.21 = (s32[4]{0:T(128)S(1)}, s32[4]{0:T(128)}, u32[]{:S(2)}) copy-start(s32[4]{0:T(128)} %copy-done.20) | copy-start | bytes 52
  719.5 49.3 %copy-start.23 = (s32[4]{0:T(128)S(1)}, s32[4]{0:T(128)}, u32[]{:S(2)}) copy-start(s32[4]{0:T(128)} %copy-done.22) | copy-start | bytes 52
  719.6 49.3 %copy-start.25 = (s32[4]{0:T(128)S(1)}, s32[4]{0:T(128)}, u32[]{:S(2)}) copy-start(s32[4]{0:T(128)} %copy-done.24) | copy-start | bytes 52
  719.6 49.2 %copy-start.27 = (s32[4]{0:T(128)S(1)}, s32[4]{0:T(128)}, u32[]{:S(2)}) copy-start(s32[4]{0:T(128)} %copy-done.26) | copy-start | bytes 52
  767.2 24.5 %collective-permute-start.17 = (f32[1024,256]{0,1:T(8,128)S(1)}, f32[1024,256]{0,1:T(8,128)}, u32[]{:S(2)}, u32[]{:S(2)}) collective-permute-start(f32[1024,256]{0,1:T(8,128)S(1)} %pad_maximum_fusion.17), channel_id=1, source_target_pairs={{0,2},{2,0},{1,3},{3,1},{4,6},{6,4},{5,7},{7,5},{8,10},{10,8},{9,1... | collective-permute-start | bytes 3145736 | tf_op jit(solution)/shard_map/ppermute | solution.py:16
  795.0 1.8 copy-start.19
  798.7 66.5 %all-gather.17.cloned.1.call-start = ((), (), s32[]{:S(2)}) async-start(), calls=%async_computation.17 | async-start | bytes 1310720 | tf_op jit(solution)/shard_map/all_gather | solution.py:78
  826.2 3.9 copy-start.10
  826.2 4.0 copy-start.30
  831.5 4.2 copy-start.12
  832.7 3.0 collective-permute-start.18
  865.2 3.9 copy-start.7
  865.2 4.0 copy-start.31
  871.7 3.0 collective-permute-start.19
  871.9 5.0 copy-start.4
  871.9 5.1 copy-start.14
  876.9 3.0 collective-permute-start.20
  877.1 2.7 copy-start.5
  883.1 1.8 copy-start.17
  (1 other events, 0.5 us)
Sparse Core Ops, SparseCore 0:
  31.4 46.0 reduce-scatter.6
  93.5 42.9 reduce-scatter.8
  203.7 42.2 reduce-scatter.10
  297.0 41.9 reduce-scatter.12
  357.1 27.2 all-gather.6
  415.3 43.0 reduce-scatter.14
  460.6 27.1 all-gather.8
  509.7 50.4 reduce-scatter.16
  577.5 27.9 all-gather.10
  672.3 27.3 all-gather.12
  798.8 27.3 all-gather.14
  837.8 27.3 all-gather.16
where the time goes:
time: 902 us; the launch traced here: 894 us
  waiting for transfers between devices  572 us (63%)
  local copies, waits for them, and re-layouts  150 us (17%)
  matrix products  100 us (11%)
  other arithmetic  40.8 us (5%)
  starting transfers between devices  16.4 us (2%)
  between operations  15.5 us (2%)
    reduce_scatter x5, waiting for transfers between devices, row_reduced(): lax.psum_scatter(complex_apply(real_part, imag_part, gathered, False), 'r...  215 us
    ppermute x21, waiting for transfers between devices, partner_2(): return lax.ppermute(block, axis, route)  168 us
    all_gather x5, waiting for transfers between devices, row_folded(): lax.all_gather(vector_half, 'row', axis=0, tiled=True)  137 us
    unnamed x77, local copies, waits for them, and re-layouts  74.2 us
    slice x5, local copies, waits for them, and re-layouts, panel_parts(): return (merged[0], merged[1])  59.3 us
    dot_general x10, matrix products, complex_apply(): lax.dot_general(imag_part, right_side, dim_numbers, preferred_element_typ...  53.9 us
    reduce_scatter x1, waiting for transfers between devices, shards(): lax.psum_scatter(partial_value, 'leaf', scatter_dimension=0, tiled=True)  50.6 us
    dot_general x10, matrix products, complex_apply(): lax.dot_general(real_part, right_side, dim_numbers, preferred_element_typ...  41.9 us
  transfers between devices with their start and end apart: 33, of which 24 were waited for; matrix products, arithmetic and copies ran while one was open for 15% of the time, Pallas kernels for 0%

commit v1 on v0

--- a/solution.py
+++ b/solution.py
@@ -16,32 +16,34 @@
     return lax.ppermute(block, axis, route)
 
 
-def complex_apply(real_part, imag_part, right_side, transpose):
-    half_cols = right_side.shape[1] // 2
-    if transpose:
-        dim_numbers = (((0,), (0,)), ((), ()))
-    else:
-        dim_numbers = (((1,), (0,)), ((), ()))
-    product_real = lax.dot_general(
-        real_part, right_side, dim_numbers, preferred_element_type=jnp.float32
-    )
-    product_imag = lax.dot_general(
-        imag_part, right_side, dim_numbers, preferred_element_type=jnp.float32
-    )
-    return jnp.concatenate(
+def turned(vector):
+    half_cols = vector.shape[1] // 2
+    return jnp.stack(
         [
-            product_real[:, :half_cols] - product_imag[:, half_cols:],
-            product_real[:, half_cols:] + product_imag[:, :half_cols],
-        ],
-        axis=1,
-    )
-
-
-def panel_parts(panel_tile):
-    merged = panel_tile.reshape(
-        2, panel_tile.shape[1], panel_tile.shape[2] * panel_tile.shape[3] * panel_tile.shape[4]
-    )
-    return (merged[0], merged[1])
+            vector,
+            jnp.concatenate([-vector[:, half_cols:], vector[:, :half_cols]], axis=1),
+        ]
+    )
+
+
+def forward_apply(panel_tile, vector):
+    positions, width = panel_tile.shape[2], panel_tile.shape[4]
+    return lax.dot_general(
+        panel_tile[:, :, :, 0, :],
+        turned(vector).reshape(2, positions, width, -1),
+        (((0, 2, 3), (0, 1, 2)), ((), ())),
+        preferred_element_type=jnp.float32,
+    )
+
+
+def transposed_apply(panel_tile, vector):
+    product = lax.dot_general(
+        panel_tile[:, :, :, 0, :],
+        turned(vector),
+        (((0, 1), (0, 1)), ((), ())),
+        preferred_element_type=jnp.float32,
+    )
+    return product.reshape(-1, vector.shape[1])
 
 
 def subgroup_gather(vector, bit_count, leaf_pos):
@@ -57,26 +59,32 @@
     return gathered
 
 
-def subgroup_sum(partial_value, bit_count, leaf_pos, slice_rows):
-    total_sum = partial_value
-    for bit_pos in range(bit_count):
-        total_sum = total_sum + partner_2(total_sum, "leaf", bit_pos)
-    position = leaf_pos & (1 << bit_count) - 1
-    return lax.dynamic_slice_in_dim(total_sum, position * slice_rows, slice_rows, 0)
+def subgroup_sum(partial_value, bit_count, leaf_pos, order):
+    rows = partial_value.shape[0] >> bit_count
+    columns = partial_value.shape[1]
+    shape = (2,) * bit_count + (rows, columns)
+    total = partial_value.reshape(shape)
+    left = list(range(bit_count))
+    for bit_pos in order:
+        axis = left[::-1].index(bit_pos)
+        mine = leaf_pos >> bit_pos & 1
+        keep = lax.dynamic_index_in_dim(total, mine, axis, keepdims=False)
+        give = lax.dynamic_index_in_dim(total, 1 - mine, axis, keepdims=False)
+        got = partner_2(give.astype(jnp.bfloat16), "leaf", bit_pos)
+        total = keep + got.astype(jnp.float32)
+        left.remove(bit_pos)
+    return total.reshape(rows, columns)
 
 
 def row_reduced(panel_tile, gathered):
-    real_part, imag_part = panel_parts(panel_tile)
-    return lax.psum_scatter(
-        complex_apply(real_part, imag_part, gathered, False), "row", scatter_dimension=0, tiled=True
+    partial_value = forward_apply(panel_tile, gathered).astype(jnp.bfloat16)
+    return lax.psum_scatter(partial_value, "row", scatter_dimension=0, tiled=True).astype(
+        jnp.float32
     )
 
 
 def row_folded(panel_tile, vector_half):
-    real_part, imag_part = panel_parts(panel_tile)
-    return complex_apply(
-        real_part, imag_part, lax.all_gather(vector_half, "row", axis=0, tiled=True), True
-    )
+    return transposed_apply(panel_tile, lax.all_gather(vector_half, "row", axis=0, tiled=True))
 
 
 def slot_ids(position, row_pos, row_size, blocks_dev, sep_blocks, has_update):
@@ -134,7 +142,6 @@
     row_pos = lax.axis_index("row")
     row_size = lax.axis_size("row")
     leaf_bits = lax.axis_size("leaf").bit_length() - 1
-    slice_rows = rhs.shape[1]
     inverses = (inv_top, inv_mid, inv_low)
     couplings = (None, couple_mid, couple_low)
     children = leaf_update
@@ -162,7 +169,7 @@
     gathered = lax.all_gather(sep_top.astype(jnp.bfloat16), "leaf", axis=0, tiled=True)
     y_top = row_reduced(inv_top, gathered)
     partial_value = row_folded(inv_top, y_top.astype(jnp.bfloat16))
-    x_top = lax.psum_scatter(partial_value, "leaf", scatter_dimension=0, tiled=True)
+    x_top = subgroup_sum(partial_value, leaf_bits, leaf_pos, range(leaf_bits))
     solutions = [x_top]
     front_rows = x_top
     for level_index in (1, 2):
@@ -174,14 +181,14 @@
             row_folded(couplings[level_index], x_update.astype(jnp.bfloat16)),
             bit_count,
             leaf_pos,
-            slice_rows,
+            range(bit_count),
         )
         reduced = saved_y[level_index] - coupled
         x_sep = subgroup_sum(
             row_folded(inverses[level_index], reduced.astype(jnp.bfloat16)),
             bit_count,
             leaf_pos,
-            slice_rows,
+            range(bit_count),
         )
         solutions.append(x_sep)
         front_rows = jnp.concatenate([x_sep, x_update], axis=0)

time: 902 us -> 679 us (0.75)
  waiting for transfers between devices: 572 us -> 423 us
  local copies, waits for them, and re-layouts: 150 us -> 42.3 us
  matrix products: 100 us -> 141 us
  other arithmetic: 40.8 us -> 30.9 us
    reduce_scatter x6 -> x5, waiting for transfers between devices: 266 us -> 134 us  [row_reduced(): lax.psum_scatter(partial_value, 'row', scatter_dimension=0, tiled=True)]
    unnamed x77 -> x41, local copies, waits for them, and re-layouts: 74.2 us -> 3.61 us
    slice x5 -> x0, local copies, waits for them, and re-layouts: 59.3 us -> none  [panel_parts(): return (merged[0], merged[1])]
    ppermute x21 -> x24, waiting for transfers between devices: 168 us -> 125 us  [partner_2(): return lax.ppermute(block, axis, route)]
    dot_general x20 -> x10, matrix products: 95.8 us -> 136 us  [the longest x5 84.5 us: forward_apply(): lax.dot_general(panel_tile[:, :, :, 0, :], turned(vector).reshape(2, posi...]
    all_gather x1, waiting for transfers between devices: 0.01 us -> 26.7 us  [shards(): lax.all_gather(sep_top.astype(jnp.bfloat16), 'leaf', axis=0, tiled=True)]
    concatenate x10 -> x5, other arithmetic: 11.9 us -> 0.5 us  [turned(): jnp.concatenate([-vector[:, half_cols:], vector[:, :half_cols]], axis=1)]
    another operation x0 -> x9, local copies, waits for them, and re-layouts: none -> 11.1 us  [turned(): jnp.stack([vector, jnp.concatenate([-vector[:, half_cols:], vector[:, :ha...]
  transfers between devices with their start and end apart: 33 -> 35, of which waited for: 24 -> 31; matrix products, arithmetic and copies ran while one was open for 15% -> 2% of each run, Pallas kernels for 0% -> 0%
where the time goes in v1:
time: 679 us; the launch traced here: 671 us
  waiting for transfers between devices  423 us (62%)
  matrix products  141 us (21%)
  local copies, waits for them, and re-layouts  42.3 us (6%)
  other arithmetic  30.9 us (5%)
  starting transfers between devices  18.8 us (3%)
  between operations  15.4 us (2%)
    all_gather x5, waiting for transfers between devices, row_folded(): lax.all_gather(vector_half, 'row', axis=0, tiled=True)  138 us
    reduce_scatter x5, waiting for transfers between devices, row_reduced(): lax.psum_scatter(partial_value, 'row', scatter_dimension=0, tiled=True)  134 us
    ppermute x24, waiting for transfers between devices, partner_2(): return lax.ppermute(block, axis, route)  125 us
    dot_general x5, matrix products, forward_apply(): lax.dot_general(panel_tile[:, :, :, 0, :], turned(vector).reshape(2, posi...  84.5 us
    dot_general x5, matrix products, transposed_apply(): lax.dot_general(panel_tile[:, :, :, 0, :], turned(vector), (((0, 1), (0,...  51.8 us
    all_gather x1, waiting for transfers between devices, shards(): lax.all_gather(sep_top.astype(jnp.bfloat16), 'leaf', axis=0, tiled=True)  26.7 us
    ppermute x24, starting transfers between devices, partner_2(): return lax.ppermute(block, axis, route)  17.7 us
  transfers between devices with their start and end apart: 35, of which 31 were waited for; matrix products, arithmetic and copies ran while one was open for 2% of the time, Pallas kernels for 0%

profile of v1, /device:TPU:0, one launch (start us, length us, event | category | flops | bytes accessed | tf_op | source)
XLA Modules:
  0.0 671.2 jit_solution(10558729055210449567)
XLA Ops:
  15.2 6.7 %fusion.63 = bf16[2048,256]{0,1:T(8,128)(2,1)} fusion(bf16[2,2048,2,512]{3,2,1,0:T(2,128)(2,1)} %bitcast.272, bf16[1,2,512,256]{2,3,1,0:T(8,128)(2,1)S(1)} %copy.48, bf16[1,2,512,256]{2,3,1,0:T(8,128)(2,1)S(1)} %copy.47), kind=kOutput, calls=%fused_computation.35 | convolution fusion | flops 2148532224 | bytes 10485760 | tf_op jit(solution)/shard_map/dot_general | solution.py:31
  22.0 29.8 %reduce-scatter.6.cloned.1.call-done = bf16[512,256]{0,1:T(8,128)(2,1)} async-done(((bf16[2048,256]{0,1:T(8,128)(2,1)}), bf16[512,256]{0,1:T(8,128)(2,1)}) %reduce-scatter.6.cloned.1.call-update) | async-done | bytes 262160 | tf_op jit(solution)/shard_map/reduce_scatter | solution.py:81
  51.8 1.7 collective-permute-done.5
  55.4 6.7 %fusion.66 = bf16[2048,256]{0,1:T(8,128)(2,1)} fusion(bf16[2,2048,2,512]{3,2,1,0:T(2,128)(2,1)} %bitcast.270, bf16[1,2,512,256]{2,3,1,0:T(8,128)(2,1)S(1)} %copy.51, bf16[1,2,512,256]{2,3,1,0:T(8,128)(2,1)S(1)} %bitcast.263), kind=kOutput, calls=%fused_computation.36 | convolution fusion | flops 2148532224 | bytes 10485760 | tf_op jit(solution)/shard_map/dot_general | solution.py:31
  63.0 25.2 %reduce-scatter.8.cloned.1.call-done = bf16[512,256]{0,1:T(8,128)(2,1)} async-done(((bf16[2048,256]{0,1:T(8,128)(2,1)}), bf16[512,256]{0,1:T(8,128)(2,1)}) %reduce-scatter.8.cloned.1.call-update) | async-done | bytes 262160 | tf_op jit(solution)/shard_map/reduce_scatter | solution.py:81
  89.2 1.5 collective-permute-start.6
  91.5 11.0 %collective-permute-done.1 = s32[4]{0:T(128)S(1)} collective-permute-done((s32[4]{0:T(128)S(1)}, s32[4]{0:T(128)S(1)}, u32[]{:S(2)}, u32[]{:S(2)}) %collective-permute-start.1) | collective-permute-done | bytes 48 | tf_op jit(solution)/shard_map/ppermute | solution.py:16
  104.9 1.5 collective-permute-done.7
  106.5 1.5 collective-permute-start.8
  109.9 10.7 %collective-permute-done.8 = bf16[1024,256]{0,1:T(8,128)(2,1)S(1)} collective-permute-done((bf16[1024,256]{0,1:T(8,128)(2,1)S(1)}, bf16[1024,256]{0,1:T(8,128)(2,1)S(1)}, u32[]{:S(2)}, u32[]{:S(2)}) %collective-permute-start.8) | collective-permute-done | bytes 524320 | tf_op jit(solution)/shard_map/ppermute | solution.py:16
  124.9 12.5 %fusion.57 = bf16[2048,256]{0,1:T(8,128)(2,1)} fusion(bf16[2,2048,4,512]{3,2,1,0:T(4,128)(2,1)} %bitcast.268, bf16[1,4,512,256]{2,3,1,0:T(8,128)(2,1)} %copy.59, bf16[1,4,512,256]{2,3,1,0:T(8,128)(2,1)S(1)} %bitcast.257), kind=kOutput, calls=%fused_computation.33 | convolution fusion | flops 4296540160 | bytes 19922944 | tf_op jit(solution)/shard_map/dot_general | solution.py:31
  137.6 26.0 %reduce-scatter.10.cloned.1.call-done = bf16[512,256]{0,1:T(8,128)(2,1)} async-done(((bf16[2048,256]{0,1:T(8,128)(2,1)}), bf16[512,256]{0,1:T(8,128)(2,1)}) %reduce-scatter.10.cloned.1.call-update) | async-done | bytes 262160 | tf_op jit(solution)/shard_map/reduce_scatter | solution.py:81
  163.7 1.7 collective-permute-done.9
  166.6 1.5 collective-permute-start.10
  169.3 11.3 %collective-permute-done.10 = bf16[1024,256]{0,1:T(8,128)(2,1)S(1)} collective-permute-done((bf16[1024,256]{0,1:T(8,128)(2,1)S(1)}, bf16[1024,256]{0,1:T(8,128)(2,1)S(1)}, u32[]{:S(2)}, u32[]{:S(2)}) %collective-permute-start.10) | collective-permute-done | bytes 524320 | tf_op jit(solution)/shard_map/ppermute | solution.py:16
  185.0 12.5 %fusion.60 = bf16[2048,256]{0,1:T(8,128)(2,1)} fusion(bf16[2,2048,4,512]{3,2,1,0:T(4,128)(2,1)} %bitcast.266, bf16[1,4,512,256]{2,3,1,0:T(8,128)(2,1)} %copy.62, bf16[1,4,512,256]{2,3,1,0:T(8,128)(2,1)S(1)} %bitcast.253), kind=kOutput, calls=%fused_computation.34 | convolution fusion | flops 4296540160 | bytes 19922944 | tf_op jit(solution)/shard_map/dot_general | solution.py:31
  198.1 25.3 %reduce-scatter.12.cloned.1.call-done = bf16[512,256]{0,1:T(8,128)(2,1)} async-done(((bf16[2048,256]{0,1:T(8,128)(2,1)}), bf16[512,256]{0,1:T(8,128)(2,1)}) %reduce-scatter.12.cloned.1.call-update) | async-done | bytes 262160 | tf_op jit(solution)/shard_map/reduce_scatter | solution.py:81
  224.4 1.5 collective-permute-start.11
  226.5 11.3 %collective-permute-done = s32[4]{0:T(128)S(1)} collective-permute-done((s32[4]{0:T(128)S(1)}, s32[4]{0:T(128)S(1)}, u32[]{:S(2)}, u32[]{:S(2)}) %collective-permute-start) | collective-permute-done | bytes 48 | tf_op jit(solution)/shard_map/ppermute | solution.py:16
  239.6 1.8 fusion.110
  241.4 26.7 %all-gather.7.cloned.1.call-done = bf16[4096,256]{1,0:T(8,128)(2,1)} async-done(((bf16[512,256]{1,0:T(8,128)(2,1)}), bf16[4096,256]{1,0:T(8,128)(2,1)}) %all-gather.7.cloned.1.call-update) | async-done | bytes 2097168 | tf_op jit(solution)/shard_map/all_gather | solution.py:169
  268.1 4.1 copy.66
  272.7 2.4 copy.67
  275.1 46.1 %fusion.69 = bf16[2048,256]{0,1:T(8,128)(2,1)} fusion(bf16[2,2048,8,512]{3,2,1,0:T(8,128)(2,1)} %bitcast.264, bf16[1,8,512,256]{2,3,1,0:T(8,128)(2,1)} %copy.67, bf16[1,8,512,256]{2,3,1,0:T(8,128)(2,1)} %copy.66), kind=kOutput, calls=%fused_computation.37 | convolution fusion | flops 8592556032 | bytes 38797312 | tf_op jit(solution)/shard_map/dot_general | solution.py:31
  321.3 27.4 %reduce-scatter.14.cloned.1.call-done = bf16[512,256]{0,1:T(8,128)(2,1)} async-done(((bf16[2048,256]{0,1:T(8,128)(2,1)}), bf16[512,256]{0,1:T(8,128)(2,1)}) %reduce-scatter.14.cloned.1.call-update) | async-done | bytes 262160 | tf_op jit(solution)/shard_map/reduce_scatter | solution.py:81
  348.8 28.0 %all-gather.9.cloned.1.call-done = bf16[2048,256]{0,1:T(8,128)(2,1)} async-done(((bf16[512,256]{0,1:T(8,128)(2,1)}), bf16[2048,256]{0,1:T(8,128)(2,1)}) %all-gather.9.cloned.1.call-update) | async-done | bytes 1048592 | tf_op jit(solution)/shard_map/all_gather | solution.py:87
  378.4 23.9 %fusion = f32[256,8,512,1]{2,0,3,1:T(8,128)} fusion(bf16[2,2048,8,512]{3,2,1,0:T(8,128)(2,1)} %bitcast.265, bf16[1,2048,256]{1,2,0:T(8,128)(2,1)S(1)} %maximum_bitcast_fusion.14, bf16[1,2048,256]{1,2,0:T(8,128)(2,1)S(1)} %bitcast.252), kind=kOutput, calls=%fused_computation | convolution fusion | flops 8594128896 | bytes 39845888 | tf_op jit(solution)/shard_map/dot_general | solution.py:40
  402.3 1.7 fusion.96
  404.1 2.6 collective-permute-done.12
  406.7 2.0 bitcast_add_fusion
  408.8 1.5 collective-permute-start.13
  410.4 12.6 %collective-permute-done.13 = bf16[2,512,256]{1,2,0:T(8,128)(2,1)} collective-permute-done((bf16[2,512,256]{1,2,0:T(8,128)(2,1)S(1)}, bf16[2,512,256]{1,2,0:T(8,128)(2,1)}, u32[]{:S(2)}, u32[]{:S(2)}) %collective-permute-start.13) | collective-permute-done | bytes 524320 | tf_op jit(solution)/shard_map/ppermute | solution.py:16
  424.2 1.5 collective-permute-start.14
  425.8 6.0 collective-permute-done.14
  431.9 1.5 collective-permute-start.15
  433.5 10.7 %collective-permute-done.15 = f32[512,256]{0,1:T(8,128)S(1)} collective-permute-done((f32[512,256]{0,1:T(8,128)S(1)}, f32[512,256]{0,1:T(8,128)S(1)}, u32[]{:S(2)}, u32[]{:S(2)}) %collective-permute-start.15) | collective-permute-done | bytes 524320 | tf_op jit(solution)/shard_map/ppermute | solution.py:16
  446.9 27.5 %all-gather.11.cloned.1.call-done = bf16[2048,256]{0,1:T(8,128)(2,1)} async-done(((bf16[512,256]{0,1:T(8,128)(2,1)}), bf16[2048,256]{0,1:T(8,128)(2,1)}) %all-gather.11.cloned.1.call-update) | async-done | bytes 1048592 | tf_op jit(solution)/shard_map/all_gather | solution.py:87
  474.3 1.4 slice_negate_fusion.4
  475.9 8.4 %fusion.6 = f32[256,4,512,1]{2,0,3,1:T(8,128)S(1)} fusion(bf16[2,2048,4,512]{3,2,1,0:T(4,128)(2,1)} %bitcast.267, bf16[1,2048,256]{1,2,0:T(8,128)(2,1)S(1)} %maximum_bitcast_fusion.15, bf16[1,2048,256]{1,2,0:T(8,128)(2,1)S(1)} %bitcast.254), kind=kOutput, calls=%fused_computation.6 | convolution fusion | flops 4299161600 | bytes 20971520 | tf_op jit(solution)/shard_map/dot_general | solution.py:40
  485.7 1.9 copy.75
  488.7 1.6 copy.76
  490.5 1.5 collective-permute-start.17
  492.0 6.8 %collective-permute-done.17 = bf16[512,256]{0,1:T(8,128)(2,1)S(1)} collective-permute-done((bf16[512,256]{0,1:T(8,128)(2,1)S(1)}, bf16[512,256]{0,1:T(8,128)(2,1)S(1)}, u32[]{:S(2)}, u32[]{:S(2)}) %collective-permute-start.17) | collective-permute-done | bytes 262176 | tf_op jit(solution)/shard_map/ppermute | solution.py:16
  499.7 27.5 %all-gather.13.cloned.1.call-done = bf16[2048,256]{0,1:T(8,128)(2,1)} async-done(((bf16[512,256]{0,1:T(8,128)(2,1)}), bf16[2048,256]{0,1:T(8,128)(2,1)}) %all-gather.13.cloned.1.call-update) | async-done | bytes 1048592 | tf_op jit(solution)/shard_map/all_gather | solution.py:87
  528.7 8.2 %fusion.4 = f32[256,4,512,1]{2,0,3,1:T(8,128)S(1)} fusion(bf16[2,2048,4,512]{3,2,1,0:T(4,128)(2,1)} %bitcast.269, bf16[1,2048,256]{1,2,0:T(8,128)(2,1)S(1)} %maximum_bitcast_fusion.16, bf16[1,2048,256]{1,2,0:T(8,128)(2,1)S(1)} %bitcast.255), kind=kOutput, calls=%fused_computation.4 | convolution fusion | flops 4299161600 | bytes 20971520 | tf_op jit(solution)/shard_map/dot_general | solution.py:40
  537.0 1.9 collective-permute-done.18
  539.1 1.5 collective-permute-start.19
  540.7 6.9 %collective-permute-done.19 = bf16[512,256]{0,1:T(8,128)(2,1)S(1)} collective-permute-done((bf16[512,256]{0,1:T(8,128)(2,1)S(1)}, bf16[512,256]{0,1:T(8,128)(2,1)S(1)}, u32[]{:S(2)}, u32[]{:S(2)}) %collective-permute-start.19) | collective-permute-done | bytes 262176 | tf_op jit(solution)/shard_map/ppermute | solution.py:16
  547.7 1.5 collective-permute-start.20
  549.4 22.9 %collective-permute-done.20 = f32[1024,256]{0,1:T(8,128)} collective-permute-done((f32[1024,256]{0,1:T(8,128)S(1)}, f32[1024,256]{0,1:T(8,128)}, u32[]{:S(2)}, u32[]{:S(2)}) %collective-permute-start.20) | collective-permute-done | bytes 1048608 | tf_op jit(solution)/shard_map/ppermute | solution.py:16
  572.2 1.4 pad_maximum_fusion.1
  573.6 1.8 copy.82
  575.5 1.7 reshape.257
  579.7 27.2 %all-gather.15.cloned.1.call-done = bf16[2048,256]{0,1:T(8,128)(2,1)} async-done(((bf16[512,256]{0,1:T(8,128)(2,1)}), bf16[2048,256]{0,1:T(8,128)(2,1)}) %all-gather.15.cloned.1.call-update) | async-done | bytes 1048592 | tf_op jit(solution)/shard_map/all_gather | solution.py:87
  606.9 1.4 slice_negate_fusion.2
  608.4 5.7 fusion.90
  614.3 1.5 collective-permute-done.21
  616.6 27.5 %all-gather.17.cloned.1.call-done = bf16[2048,256]{0,1:T(8,128)(2,1)} async-done(((bf16[512,256]{0,1:T(8,128)(2,1)}), bf16[2048,256]{0,1:T(8,128)(2,1)}) %all-gather.17.cloned.1.call-update) | async-done | bytes 1048592 | tf_op jit(solution)/shard_map/all_gather | solution.py:87
  645.7 5.7 fusion.93
  651.5 1.5 collective-permute-done.22
  654.6 1.6 copy.89
  657.3 1.4 pad_maximum_fusion.2
  658.7 1.8 copy.88
  660.5 1.7 reshape.259
  (210 shorter events, 53.6 us)
Async XLA Ops:
  7.2 3.5 copy-start.16
  7.2 44.6 %reduce-scatter.6.cloned.1.call-start = ((), (), s32[]{:S(2)}) async-start(), calls=%async_computation.5 | async-start | bytes 1310720 | tf_op jit(solution)/shard_map/reduce_scatter | solution.py:81
  8.0 2.2 copy-start.17
  8.0 2.1 collective-permute-start.2
  8.5 2.1 collective-permute-start.3
  12.4 1.6 collective-permute-start.4
  22.0 66.2 %reduce-scatter.8.cloned.1.call-start = ((), (), s32[]{:S(2)}) async-start(), calls=%async_computation.6 | async-start | bytes 1310720 | tf_op jit(solution)/shard_map/reduce_scatter | solution.py:81
  51.8 3.0 copy-start.6
  51.8 1.7 collective-permute-start.5
  62.2 101.5 %reduce-scatter.10.cloned.1.call-start = ((), (), s32[]{:S(2)}) async-start(), calls=%async_computation.7 | async-start | bytes 1310720 | tf_op jit(solution)/shard_map/reduce_scatter | solution.py:81
  89.2 13.5 %collective-permute-start.6 = (f32[512,256]{0,1:T(8,128)S(1)}, f32[512,256]{0,1:T(8,128)S(1)}, u32[]{:S(2)}, u32[]{:S(2)}) collective-permute-start(f32[512,256]{0,1:T(8,128)S(1)} %convert_subtract_fusion.1), channel_id=1, source_target_pairs={{0,2},{2,0},{1,3},{3,1},{4,6},{6,4},{5,7},{7,5},{8,10},{10,8},{9,1... | collective-permute-start | bytes 1572872 | tf_op jit(solution)/shard_map/ppermute | solution.py:16
  90.7 11.9 %collective-permute-start.1 = (s32[4]{0:T(128)S(1)}, s32[4]{0:T(128)S(1)}, u32[]{:S(2)}, u32[]{:S(2)}) collective-permute-start(s32[4]{0:T(128)S(1)} %get-tuple-element.34), channel_id=1, source_target_pairs={{0,2},{2,0},{1,3},{3,1},{4,6},{6,4},{5,7},{7,5},{8,10},{10,8},{9,1... | collective-permute-start | bytes 56 | tf_op jit(solution)/shard_map/ppermute | solution.py:16
  104.8 1.6 collective-permute-start.7
  106.4 1.7 copy-start.15
  106.5 14.0 %collective-permute-start.8 = (bf16[1024,256]{0,1:T(8,128)(2,1)S(1)}, bf16[1024,256]{0,1:T(8,128)(2,1)S(1)}, u32[]{:S(2)}, u32[]{:S(2)}) collective-permute-start(bf16[1024,256]{0,1:T(8,128)(2,1)S(1)} %maximum_select_fusion.8), channel_id=1, source_target_pairs={{0,2},{2,0},{1,3},{3,1},{4,6},{6,4},{5,7},{7,5},{8,10},{10,8},{9,1... | collective-permute-start | bytes 1572872 | tf_op jit(solution)/shard_map/ppermute | solution.py:16
  123.4 1.5 copy-start.13
  137.4 86.0 %reduce-scatter.12.cloned.1.call-start = ((), (), s32[]{:S(2)}) async-start(), calls=%async_computation.8 | async-start | bytes 1310720 | tf_op jit(solution)/shard_map/reduce_scatter | solution.py:81
  163.7 1.7 collective-permute-start.9
  166.6 14.0 %collective-permute-start.10 = (bf16[1024,256]{0,1:T(8,128)(2,1)S(1)}, bf16[1024,256]{0,1:T(8,128)(2,1)S(1)}, u32[]{:S(2)}, u32[]{:S(2)}) collective-permute-start(bf16[1024,256]{0,1:T(8,128)(2,1)S(1)} %maximum_select_fusion.10), channel_id=1, source_target_pairs={{0,2},{2,0},{1,3},{3,1},{4,6},{6,4},{5,7},{7,5},{8,10},{10,8},{9,1... | collective-permute-start | bytes 1572872 | tf_op jit(solution)/shard_map/ppermute | solution.py:16
  183.5 1.5 copy-start.9
  197.4 70.7 %all-gather.7.cloned.1.call-start = ((), (), s32[]{:S(2)}) async-start(), calls=%async_computation.9 | async-start | bytes 2359296 | tf_op jit(solution)/shard_map/all_gather | solution.py:169
  224.4 13.5 %collective-permute-start.11 = (f32[512,256]{0,1:T(8,128)S(1)}, f32[512,256]{0,1:T(8,128)S(1)}, u32[]{:S(2)}, u32[]{:S(2)}) collective-permute-start(f32[512,256]{0,1:T(8,128)S(1)} %convert_subtract_fusion), channel_id=1, source_target_pairs={{0,4},{4,0},{1,5},{5,1},{2,6},{6,2},{3,7},{7,3},{8,12},{12,8},{9,1... | collective-permute-start | bytes 1572872 | tf_op jit(solution)/shard_map/ppermute | solution.py:16
  225.9 11.9 %collective-permute-start = (s32[4]{0:T(128)S(1)}, s32[4]{0:T(128)S(1)}, u32[]{:S(2)}, u32[]{:S(2)}) collective-permute-start(s32[4]{0:T(128)S(1)} %get-tuple-element.32), channel_id=1, source_target_pairs={{0,4},{4,0},{1,5},{5,1},{2,6},{6,2},{3,7},{7,3},{8,12},{12,8},{9,1... | collective-permute-start | bytes 56 | tf_op jit(solution)/shard_map/ppermute | solution.py:16
  241.4 107.3 %reduce-scatter.14.cloned.1.call-start = ((), (), s32[]{:S(2)}) async-start(), calls=%async_computation.10 | async-start | bytes 1310720 | tf_op jit(solution)/shard_map/reduce_scatter | solution.py:81
  268.1 4.1 copy-start
  321.3 55.5 %all-gather.9.cloned.1.call-start = ((), (), s32[]{:S(2)}) async-start(), calls=%async_computation.11 | async-start | bytes 1310720 | tf_op jit(solution)/shard_map/all_gather | solution.py:87
  348.8 125.6 %all-gather.11.cloned.1.call-start = ((), (), s32[]{:S(2)}) async-start(), calls=%async_computation.12 | async-start | bytes 1310720 | tf_op jit(solution)/shard_map/all_gather | solution.py:87
  376.8 1.5 copy-start.8
  404.0 2.7 collective-permute-start.12
  408.8 14.1 %collective-permute-start.13 = (bf16[2,512,256]{1,2,0:T(8,128)(2,1)S(1)}, bf16[2,512,256]{1,2,0:T(8,128)(2,1)}, u32[]{:S(2)}, u32[]{:S(2)}) collective-permute-start(bf16[2,512,256]{1,2,0:T(8,128)(2,1)S(1)} %fusion.103), channel_id=1, source_target_pairs={{0,2},{2,0},{1,3},{3,1},{4,6},{6,4},{5,7},{7,5},{8,10},{10,8},{9,1... | collective-permute-start | bytes 1572872 | tf_op jit(solution)/shard_map/ppermute | solution.py:16
  424.2 7.6 %collective-permute-start.14 = (bf16[512,256]{0,1:T(8,128)(2,1)S(1)}, bf16[512,256]{0,1:T(8,128)(2,1)S(1)}, u32[]{:S(2)}, u32[]{:S(2)}) collective-permute-start(bf16[512,256]{0,1:T(8,128)(2,1)S(1)} %fusion.113), channel_id=1, source_target_pairs={{0,4},{4,0},{1,5},{5,1},{2,6},{6,2},{3,7},{7,3},{8,12},{12,8},{9,1... | collective-permute-start | bytes 786440 | tf_op jit(solution)/shard_map/ppermute | solution.py:16
  431.9 12.8 %copy-start.3 = (f32[512,256]{0,1:T(8,128)}, f32[512,256]{0,1:T(8,128)S(1)}, u32[]{:S(2)}) copy-start(f32[512,256]{0,1:T(8,128)S(1)} %bitcast_add_fusion.8) | copy-start | bytes 1572868
  431.9 12.3 %collective-permute-start.15 = (f32[512,256]{0,1:T(8,128)S(1)}, f32[512,256]{0,1:T(8,128)S(1)}, u32[]{:S(2)}, u32[]{:S(2)}) collective-permute-start(f32[512,256]{0,1:T(8,128)S(1)} %bitcast_add_fusion.8), channel_id=1, source_target_pairs={{0,4},{4,0},{1,5},{5,1},{2,6},{6,2},{3,7},{7,3},{8,12},{12,8},{9,1... | collective-permute-start | bytes 1572872 | tf_op jit(solution)/shard_map/ppermute | solution.py:16
  446.8 80.3 %all-gather.13.cloned.1.call-start = ((), (), s32[]{:S(2)}) async-start(), calls=%async_computation.13 | async-start | bytes 1310720 | tf_op jit(solution)/shard_map/all_gather | solution.py:87
  474.3 1.5 copy-start.10
  484.2 1.5 copy-start.5
  485.2 5.0 collective-permute-start.16
  490.2 8.5 %copy-start.7 = (bf16[512,256]{0,1:T(8,128)(2,1)S(1)}, bf16[512,256]{0,1:T(8,128)(2,1)}, u32[]{:S(2)}) copy-start(bf16[512,256]{0,1:T(8,128)(2,1)} %reduce-scatter.10.cloned.1.call-done) | copy-start | bytes 786436
  490.5 8.3 %collective-permute-start.17 = (bf16[512,256]{0,1:T(8,128)(2,1)S(1)}, bf16[512,256]{0,1:T(8,128)(2,1)S(1)}, u32[]{:S(2)}, u32[]{:S(2)}) collective-permute-start(bf16[512,256]{0,1:T(8,128)(2,1)S(1)} %fusion.114), channel_id=1, source_target_pairs={{0,2},{2,0},{1,3},{3,1},{4,6},{6,4},{5,7},{7,5},{8,10},{10,8},{9,1... | collective-permute-start | bytes 786440 | tf_op jit(solution)/shard_map/ppermute | solution.py:16
  499.6 107.3 %all-gather.15.cloned.1.call-start = ((), (), s32[]{:S(2)}) async-start(), calls=%async_computation.14 | async-start | bytes 1310720 | tf_op jit(solution)/shard_map/all_gather | solution.py:87
  527.1 1.5 copy-start.11
  536.9 2.0 collective-permute-start.18
  539.1 8.4 %collective-permute-start.19 = (bf16[512,256]{0,1:T(8,128)(2,1)S(1)}, bf16[512,256]{0,1:T(8,128)(2,1)S(1)}, u32[]{:S(2)}, u32[]{:S(2)}) collective-permute-start(bf16[512,256]{0,1:T(8,128)(2,1)S(1)} %fusion.115), channel_id=1, source_target_pairs={{0,2},{2,0},{1,3},{3,1},{4,6},{6,4},{5,7},{7,5},{8,10},{10,8},{9,1... | collective-permute-start | bytes 786440 | tf_op jit(solution)/shard_map/ppermute | solution.py:16
  547.7 24.5 %collective-permute-start.20 = (f32[1024,256]{0,1:T(8,128)S(1)}, f32[1024,256]{0,1:T(8,128)}, u32[]{:S(2)}, u32[]{:S(2)}) collective-permute-start(f32[1024,256]{0,1:T(8,128)S(1)} %pad_maximum_fusion.10), channel_id=1, source_target_pairs={{0,2},{2,0},{1,3},{3,1},{4,6},{6,4},{5,7},{7,5},{8,10},{10,8},{9,1... | collective-permute-start | bytes 3145736 | tf_op jit(solution)/shard_map/ppermute | solution.py:16
  579.4 64.8 %all-gather.17.cloned.1.call-start = ((), (), s32[]{:S(2)}) async-start(), calls=%async_computation.15 | async-start | bytes 1310720 | tf_op jit(solution)/shard_map/all_gather | solution.py:87
  606.9 1.5 copy-start.12
  614.2 1.6 collective-permute-start.21
  644.1 1.5 copy-start.14
  651.4 3.1 copy-start.4
  651.4 1.6 collective-permute-start.22
  653.1 1.3 copy-start.1
  654.3 3.0 collective-permute-start.23
  654.6 2.7 copy-start.2
  660.5 1.8 copy-start.18
Sparse Core Ops, SparseCore 0:
  22.1 29.6 reduce-scatter.5
  62.3 25.7 reduce-scatter.7
  137.5 26.1 reduce-scatter.9
  197.6 25.7 reduce-scatter.11
  241.5 26.5 all-gather.6
  321.4 27.2 reduce-scatter.13
  350.3 26.4 all-gather.8
  446.9 27.3 all-gather.10
  499.7 27.3 all-gather.12
  579.5 27.3 all-gather.14
  616.7 27.3 all-gather.16

commit v2 on v1

--- a/solution.py
+++ b/solution.py
@@ -46,34 +46,61 @@
     return product.reshape(-1, vector.shape[1])
 
 
-def subgroup_gather(vector, bit_count, leaf_pos):
-    gathered = vector
-    for bit_pos in range(bit_count):
+def gather_in_order(vector, order, leaf_pos):
+    bit_count = len(order)
+    gathered = vector[None]
+    done = []
+    for bit_pos in order:
         partner = partner_2(gathered, "leaf", bit_pos)
+        higher = [pos for pos in done if pos > bit_pos]
+        done.append(bit_pos)
+        outer = 1 << len(higher)
+        mine = gathered.reshape(outer, 1, -1, *vector.shape)
+        theirs = partner.reshape(mine.shape)
         upper_half = leaf_pos >> bit_pos & 1 == 1
         gathered = jnp.where(
             upper_half,
-            jnp.concatenate([partner, gathered], axis=0),
-            jnp.concatenate([gathered, partner], axis=0),
-        )
-    return gathered
-
-
-def subgroup_sum(partial_value, bit_count, leaf_pos, order):
-    rows = partial_value.shape[0] >> bit_count
-    columns = partial_value.shape[1]
-    shape = (2,) * bit_count + (rows, columns)
-    total = partial_value.reshape(shape)
-    left = list(range(bit_count))
+            jnp.concatenate([theirs, mine], axis=1),
+            jnp.concatenate([mine, theirs], axis=1),
+        ).reshape(-1, *vector.shape)
+    return gathered.reshape((1 << bit_count) * vector.shape[0], vector.shape[1])
+
+
+def subgroup_gather(vector, bit_count, leaf_pos):
+    if bit_count < 3:
+        return gather_in_order(vector, list(range(bit_count))[::-1], leaf_pos)
+    outer_bits = list(range(1, bit_count))
+    half_cols = vector.shape[1] // 2
+    first = gather_in_order(vector[:, :half_cols], outer_bits + [0], leaf_pos)
+    second = gather_in_order(vector[:, half_cols:], outer_bits[::-1] + [0], leaf_pos)
+    return jnp.concatenate([first, second], axis=1)
+
+
+def halved_sum(total, order, leaf_pos, left):
     for bit_pos in order:
-        axis = left[::-1].index(bit_pos)
+        axis = left.index(bit_pos)
         mine = leaf_pos >> bit_pos & 1
         keep = lax.dynamic_index_in_dim(total, mine, axis, keepdims=False)
         give = lax.dynamic_index_in_dim(total, 1 - mine, axis, keepdims=False)
         got = partner_2(give.astype(jnp.bfloat16), "leaf", bit_pos)
         total = keep + got.astype(jnp.float32)
-        left.remove(bit_pos)
-    return total.reshape(rows, columns)
+        left = [pos for pos in left if pos != bit_pos]
+    return total
+
+
+def subgroup_sum(partial_value, bit_count, leaf_pos):
+    rows = partial_value.shape[0] >> bit_count
+    columns = partial_value.shape[1]
+    total = partial_value.reshape((2,) * bit_count + (rows, columns))
+    left = list(range(bit_count))[::-1]
+    if bit_count < 3:
+        return halved_sum(total, left[::-1], leaf_pos, left)
+    total = halved_sum(total, [0], leaf_pos, left)
+    left = left[:-1]
+    half_cols = columns // 2
+    first = halved_sum(total[..., :half_cols], left, leaf_pos, left)
+    second = halved_sum(total[..., half_cols:], left[::-1], leaf_pos, left)
+    return jnp.concatenate([first, second], axis=1)
 
 
 def row_reduced(panel_tile, gathered):
@@ -98,7 +125,8 @@
 
 def extend_add(child_rows, targets, rhs_part, bit_count, has_update, leaf_pos, row_pos, row_size):
     bit_pos = bit_count - 1
-    partner_rows, partner_targets = partner_2((child_rows, targets), "leaf", bit_pos)
+    partner_targets = partner_2(targets, "leaf", bit_pos)
+    partner_rows = partner_2(child_rows.astype(jnp.bfloat16), "leaf", bit_pos).astype(jnp.float32)
     blocks_dev = targets.shape[0]
     group_size = 1 << bit_count
     position = leaf_pos & group_size - 1
@@ -117,7 +145,7 @@
 
 def extend_down(front_rows, targets, bit_count, leaf_pos, row_pos, row_size):
     bit_pos = bit_count - 1
-    partner_rows = partner_2(front_rows, "leaf", bit_pos)
+    partner_rows = partner_2(front_rows.astype(jnp.bfloat16), "leaf", bit_pos).astype(jnp.float32)
     blocks_dev = targets.shape[0]
     has_update = front_rows.shape[0] > blocks_dev * BLOCK
     group_size = 1 << bit_count
@@ -166,10 +194,10 @@
     sep_top, unused_rows = extend_add(
         children, block_map[0], rhs[0], leaf_bits, False, leaf_pos, row_pos, row_size
     )
-    gathered = lax.all_gather(sep_top.astype(jnp.bfloat16), "leaf", axis=0, tiled=True)
+    gathered = subgroup_gather(sep_top.astype(jnp.bfloat16), leaf_bits, leaf_pos)
     y_top = row_reduced(inv_top, gathered)
     partial_value = row_folded(inv_top, y_top.astype(jnp.bfloat16))
-    x_top = subgroup_sum(partial_value, leaf_bits, leaf_pos, range(leaf_bits))
+    x_top = subgroup_sum(partial_value, leaf_bits, leaf_pos)
     solutions = [x_top]
     front_rows = x_top
     for level_index in (1, 2):
@@ -181,14 +209,12 @@
             row_folded(couplings[level_index], x_update.astype(jnp.bfloat16)),
             bit_count,
             leaf_pos,
-            range(bit_count),
         )
         reduced = saved_y[level_index] - coupled
         x_sep = subgroup_sum(
             row_folded(inverses[level_index], reduced.astype(jnp.bfloat16)),
             bit_count,
             leaf_pos,
-            range(bit_count),
         )
         solutions.append(x_sep)
         front_rows = jnp.concatenate([x_sep, x_update], axis=0)

time: 679 us -> 586 us (0.86)
  waiting for transfers between devices: 423 us -> 351 us
  matrix products: 141 us -> 114 us
  starting transfers between devices: 18.8 us -> 28.2 us
    ppermute x24 -> x32, waiting for transfers between devices: 125 us -> 84.1 us  [partner_2(): return lax.ppermute(block, axis, route)]
    all_gather x1 -> x0, waiting for transfers between devices: 26.7 us -> none  [shards(): lax.all_gather(sep_top.astype(jnp.bfloat16), 'leaf', axis=0, tiled=True)]
    dot_general x5, matrix products: 84.5 us -> 57.9 us  [forward_apply(): lax.dot_general(panel_tile[:, :, :, 0, :], turned(vector).reshape(2, posi...]
    ppermute x24 -> x32, starting transfers between devices: 17.7 us -> 26.5 us  [partner_2(): return lax.ppermute(block, axis, route)]
    another operation x9 -> x4, local copies, waits for them, and re-layouts: 11.1 us -> 3.07 us  [turned(): jnp.stack([vector, jnp.concatenate([-vector[:, half_cols:], vector[:, :ha...]
  transfers between devices with their start and end apart: 35 -> 42, of which waited for: 31 -> 34; matrix products, arithmetic and copies ran while one was open for 2% -> 3% of each run, Pallas kernels for 0% -> 0%
where the time goes in v2:
time: 586 us; the launch traced here: 579 us
  waiting for transfers between devices  351 us (60%)
  matrix products  114 us (19%)
  local copies, waits for them, and re-layouts  40.2 us (7%)
  other arithmetic  29.6 us (5%)
  starting transfers between devices  28.2 us (5%)
  between operations  15.8 us (3%)
    all_gather x5, waiting for transfers between devices, row_folded(): lax.all_gather(vector_half, 'row', axis=0, tiled=True)  136 us
    reduce_scatter x5, waiting for transfers between devices, row_reduced(): lax.psum_scatter(partial_value, 'row', scatter_dimension=0, tiled=True)  130 us
    ppermute x32, waiting for transfers between devices, partner_2(): return lax.ppermute(block, axis, route)  84.1 us
    dot_general x5, matrix products, forward_apply(): lax.dot_general(panel_tile[:, :, :, 0, :], turned(vector).reshape(2, posi...  57.9 us
    dot_general x5, matrix products, transposed_apply(): lax.dot_general(panel_tile[:, :, :, 0, :], turned(vector), (((0, 1), (0,...  51.7 us
    ppermute x32, starting transfers between devices, partner_2(): return lax.ppermute(block, axis, route)  26.5 us
  transfers between devices with their start and end apart: 42, of which 34 were waited for; matrix products, arithmetic and copies ran while one was open for 3% of the time, Pallas kernels for 0%

profile of v2, /device:TPU:0, one launch (start us, length us, event | category | flops | bytes accessed | tf_op | source)
XLA Modules:
  0.0 578.5 jit_solution(14583329810889563801)
XLA Ops:
  15.6 6.7 %fusion.67 = bf16[2048,256]{0,1:T(8,128)(2,1)} fusion(bf16[2,2048,2,512]{3,2,1,0:T(2,128)(2,1)} %bitcast.316, bf16[1,2,512,256]{2,3,1,0:T(8,128)(2,1)S(1)} %copy.43, bf16[1,2,512,256]{2,3,1,0:T(8,128)(2,1)S(1)} %fusion.173), kind=kOutput, calls=%fused_computation.39 | convolution fusion | flops 2148532224 | bytes 10485760 | tf_op jit(solution)/shard_map/dot_general | solution.py:31
  22.4 30.0 %reduce-scatter.6.cloned.1.call-done = bf16[512,256]{0,1:T(8,128)(2,1)} async-done(((bf16[2048,256]{0,1:T(8,128)(2,1)}), bf16[512,256]{0,1:T(8,128)(2,1)}) %reduce-scatter.6.cloned.1.call-update) | async-done | bytes 262160 | tf_op jit(solution)/shard_map/reduce_scatter | solution.py:108
  52.4 1.7 collective-permute-done.5
  57.0 6.7 %fusion.70 = bf16[2048,256]{0,1:T(8,128)(2,1)} fusion(bf16[2,2048,2,512]{3,2,1,0:T(2,128)(2,1)} %bitcast.314, bf16[1,2,512,256]{2,3,1,0:T(8,128)(2,1)S(1)} %copy.46, bf16[1,2,512,256]{2,3,1,0:T(8,128)(2,1)S(1)} %fusion.172), kind=kOutput, calls=%fused_computation.40 | convolution fusion | flops 2148532224 | bytes 10485760 | tf_op jit(solution)/shard_map/dot_general | solution.py:31
  64.0 1.5 collective-permute-start.1
  66.1 23.6 %reduce-scatter.8.cloned.1.call-done = bf16[512,256]{0,1:T(8,128)(2,1)} async-done(((bf16[2048,256]{0,1:T(8,128)(2,1)}), bf16[512,256]{0,1:T(8,128)(2,1)}) %reduce-scatter.8.cloned.1.call-update) | async-done | bytes 262160 | tf_op jit(solution)/shard_map/reduce_scatter | solution.py:108
  90.7 1.5 collective-permute-start.6
  92.6 5.8 %collective-permute-done.6 = bf16[512,256]{0,1:T(8,128)(2,1)S(1)} collective-permute-done((bf16[512,256]{0,1:T(8,128)(2,1)S(1)}, bf16[512,256]{0,1:T(8,128)(2,1)S(1)}, u32[]{:S(2)}, u32[]{:S(2)}) %collective-permute-start.6) | collective-permute-done | bytes 262176 | tf_op jit(solution)/shard_map/ppermute | solution.py:16
  100.6 1.5 collective-permute-start.7
  102.1 5.3 collective-permute-done.7
  107.7 1.8 collective-permute-done.8
  112.8 12.4 %fusion.61 = bf16[2048,256]{0,1:T(8,128)(2,1)} fusion(bf16[2,2048,4,512]{3,2,1,0:T(4,128)(2,1)} %bitcast.312, bf16[1,4,512,256]{2,3,1,0:T(8,128)(2,1)} %copy.54, bf16[1,4,512,256]{2,3,1,0:T(8,128)(2,1)S(1)} %bitcast.293), kind=kOutput, calls=%fused_computation.37 | convolution fusion | flops 4296540160 | bytes 19922944 | tf_op jit(solution)/shard_map/dot_general | solution.py:31
  125.8 26.2 %reduce-scatter.10.cloned.1.call-done = bf16[512,256]{0,1:T(8,128)(2,1)} async-done(((bf16[2048,256]{0,1:T(8,128)(2,1)}), bf16[512,256]{0,1:T(8,128)(2,1)}) %reduce-scatter.10.cloned.1.call-update) | async-done | bytes 262160 | tf_op jit(solution)/shard_map/reduce_scatter | solution.py:108
  153.4 6.4 %collective-permute-done.9 = bf16[1,512,256]{1,2,0:T(8,128)(2,1)S(1)} collective-permute-done((bf16[1,512,256]{1,2,0:T(8,128)(2,1)}, bf16[1,512,256]{1,2,0:T(8,128)(2,1)S(1)}, u32[]{:S(2)}, u32[]{:S(2)}) %collective-permute-start.9) | collective-permute-done | bytes 262176 | tf_op jit(solution)/shard_map/ppermute | solution.py:16
  165.1 12.4 %fusion.64 = bf16[2048,256]{0,1:T(8,128)(2,1)} fusion(bf16[2,2048,4,512]{3,2,1,0:T(4,128)(2,1)} %bitcast.310, bf16[1,4,512,256]{2,3,1,0:T(8,128)(2,1)} %copy.59, bf16[1,4,512,256]{2,3,1,0:T(8,128)(2,1)S(1)} %bitcast.261), kind=kOutput, calls=%fused_computation.38 | convolution fusion | flops 4296540160 | bytes 19922944 | tf_op jit(solution)/shard_map/dot_general | solution.py:31
  178.2 25.6 %reduce-scatter.12.cloned.1.call-done = bf16[512,256]{0,1:T(8,128)(2,1)} async-done(((bf16[2048,256]{0,1:T(8,128)(2,1)}), bf16[512,256]{0,1:T(8,128)(2,1)}) %reduce-scatter.12.cloned.1.call-update) | async-done | bytes 262160 | tf_op jit(solution)/shard_map/reduce_scatter | solution.py:108
  204.9 1.6 collective-permute-start.11
  207.0 5.7 collective-permute-done
  215.7 1.5 collective-permute-start.15
  217.2 1.5 collective-permute-start.12
  218.7 2.0 collective-permute-done.15
  220.8 1.5 collective-permute-start.16
  223.9 3.9 collective-permute-done.16
  228.2 1.8 collective-permute-done.13
  233.4 19.6 %fusion.73 = bf16[2048,256]{0,1:T(8,128)(2,1)} fusion(bf16[2,2048,8,512]{3,2,1,0:T(8,128)(2,1)} %bitcast.308, bf16[1,8,512,128]{2,3,1,0:T(8,128)(2,1)S(1)} %bitcast.287, bf16[1,8,512,128]{2,3,1,0:T(8,128)(2,1)S(1)} %neg.39, bf16[1,8,512,128]{2,3,1,0:T(8,128)(2,1)S(1)} %bitcast.263), kind=kOutput, calls=%fused_computation.41 | convolution fusion | flops 8607236096 | bytes 37748736 | tf_op jit(solution)/shard_map/dot_general | solution.py:31
  253.0 25.0 %reduce-scatter.14.cloned.1.call-done = bf16[512,256]{0,1:T(8,128)(2,1)} async-done(((bf16[2048,256]{0,1:T(8,128)(2,1)}), bf16[512,256]{0,1:T(8,128)(2,1)}) %reduce-scatter.14.cloned.1.call-update) | async-done | bytes 262160 | tf_op jit(solution)/shard_map/reduce_scatter | solution.py:108
  278.3 27.7 %all-gather.6.cloned.1.call-done = bf16[2048,256]{0,1:T(8,128)(2,1)} async-done(((bf16[512,256]{0,1:T(8,128)(2,1)}), bf16[2048,256]{0,1:T(8,128)(2,1)}) %all-gather.6.cloned.1.call-update) | async-done | bytes 1048592 | tf_op jit(solution)/shard_map/all_gather | solution.py:114
  307.5 23.9 %fusion = f32[256,8,512,1]{2,0,3,1:T(8,128)} fusion(bf16[2,2048,8,512]{3,2,1,0:T(8,128)(2,1)} %bitcast.309, bf16[1,2048,256]{1,2,0:T(8,128)(2,1)S(1)} %maximum_bitcast_fusion.14, bf16[1,2048,256]{1,2,0:T(8,128)(2,1)S(1)} %bitcast.288), kind=kOutput, calls=%fused_computation | convolution fusion | flops 8594128896 | bytes 39845888 | tf_op jit(solution)/shard_map/dot_general | solution.py:40
  331.4 1.7 fusion.100
  333.2 2.6 collective-permute-done.18
  335.9 1.9 bitcast_add_fusion
  338.0 1.5 collective-permute-start.21
  339.6 1.5 collective-permute-start.19
  341.1 5.3 collective-permute-done.21
  346.6 1.5 collective-permute-start.22
  348.2 1.5 collective-permute-start.20
  349.8 1.8 collective-permute-done.22
  351.6 1.6 collective-permute-done.20
  354.6 5.2 collective-permute-done.23
  362.7 26.3 %all-gather.8.cloned.1.call-done = bf16[2048,256]{0,1:T(8,128)(2,1)} async-done(((bf16[512,256]{0,1:T(8,128)(2,1)}), bf16[2048,256]{0,1:T(8,128)(2,1)}) %all-gather.8.cloned.1.call-update) | async-done | bytes 1048592 | tf_op jit(solution)/shard_map/all_gather | solution.py:114
  390.6 8.2 %fusion.6 = f32[256,4,512,1]{2,0,3,1:T(8,128)S(1)} fusion(bf16[2,2048,4,512]{3,2,1,0:T(4,128)(2,1)} %bitcast.311, bf16[1,2048,256]{1,2,0:T(8,128)(2,1)S(1)} %maximum_bitcast_fusion.15, bf16[1,2048,256]{1,2,0:T(8,128)(2,1)S(1)} %bitcast.290), kind=kOutput, calls=%fused_computation.6 | convolution fusion | flops 4299161600 | bytes 20971520 | tf_op jit(solution)/shard_map/dot_general | solution.py:40
  400.3 1.9 copy.76
  403.2 1.6 copy.77
  406.1 1.5 collective-permute-start.25
  407.6 6.8 %collective-permute-done.25 = bf16[512,256]{0,1:T(8,128)(2,1)S(1)} collective-permute-done((bf16[512,256]{0,1:T(8,128)(2,1)S(1)}, bf16[512,256]{0,1:T(8,128)(2,1)S(1)}, u32[]{:S(2)}, u32[]{:S(2)}) %collective-permute-start.25) | collective-permute-done | bytes 262176 | tf_op jit(solution)/shard_map/ppermute | solution.py:16
  415.3 27.5 %all-gather.10.cloned.1.call-done = bf16[2048,256]{0,1:T(8,128)(2,1)} async-done(((bf16[512,256]{0,1:T(8,128)(2,1)}), bf16[2048,256]{0,1:T(8,128)(2,1)}) %all-gather.10.cloned.1.call-update) | async-done | bytes 1048592 | tf_op jit(solution)/shard_map/all_gather | solution.py:114
  444.3 8.2 %fusion.4 = f32[256,4,512,1]{2,0,3,1:T(8,128)S(1)} fusion(bf16[2,2048,4,512]{3,2,1,0:T(4,128)(2,1)} %bitcast.313, bf16[1,2048,256]{1,2,0:T(8,128)(2,1)S(1)} %maximum_bitcast_fusion.16, bf16[1,2048,256]{1,2,0:T(8,128)(2,1)S(1)} %bitcast.289), kind=kOutput, calls=%fused_computation.4 | convolution fusion | flops 4299161600 | bytes 20971520 | tf_op jit(solution)/shard_map/dot_general | solution.py:40
  453.9 1.9 copy.80
  456.9 1.6 copy.81
  459.8 1.5 collective-permute-start.27
  461.4 6.8 %collective-permute-done.27 = bf16[512,256]{0,1:T(8,128)(2,1)S(1)} collective-permute-done((bf16[512,256]{0,1:T(8,128)(2,1)S(1)}, bf16[512,256]{0,1:T(8,128)(2,1)S(1)}, u32[]{:S(2)}, u32[]{:S(2)}) %collective-permute-start.27) | collective-permute-done | bytes 262176 | tf_op jit(solution)/shard_map/ppermute | solution.py:16
  468.3 1.5 collective-permute-start.28
  470.0 11.4 %collective-permute-done.28 = bf16[1024,256]{0,1:T(8,128)(2,1)S(1)} collective-permute-done((bf16[1024,256]{0,1:T(8,128)(2,1)S(1)}, bf16[1024,256]{0,1:T(8,128)(2,1)S(1)}, u32[]{:S(2)}, u32[]{:S(2)}) %collective-permute-start.28) | collective-permute-done | bytes 524320 | tf_op jit(solution)/shard_map/ppermute | solution.py:16
  481.6 1.8 copy.84
  483.5 1.7 reshape.845
  487.7 27.2 %all-gather.12.cloned.1.call-done = bf16[2048,256]{0,1:T(8,128)(2,1)} async-done(((bf16[512,256]{0,1:T(8,128)(2,1)}), bf16[2048,256]{0,1:T(8,128)(2,1)}) %all-gather.12.cloned.1.call-update) | async-done | bytes 1048592 | tf_op jit(solution)/shard_map/all_gather | solution.py:114
  516.4 5.7 fusion.94
  522.3 1.5 collective-permute-done.29
  524.7 27.5 %all-gather.14.cloned.1.call-done = bf16[2048,256]{0,1:T(8,128)(2,1)} async-done(((bf16[512,256]{0,1:T(8,128)(2,1)}), bf16[2048,256]{0,1:T(8,128)(2,1)}) %all-gather.14.cloned.1.call-update) | async-done | bytes 1048592 | tf_op jit(solution)/shard_map/all_gather | solution.py:114
  553.7 5.7 fusion.97
  559.6 1.5 collective-permute-done.30
  562.4 1.6 copy.90
  565.7 1.8 copy.89
  567.5 1.7 reshape.847
  (242 shorter events, 66.5 us)
Async XLA Ops:
  7.2 45.3 %reduce-scatter.6.cloned.1.call-start = ((), (), s32[]{:S(2)}) async-start(), calls=%async_computation.5 | async-start | bytes 1310720 | tf_op jit(solution)/shard_map/reduce_scatter | solution.py:108
  8.0 3.4 copy-start.15
  8.0 3.3 collective-permute-start.2
  9.6 1.9 copy-start.8
  9.6 1.8 collective-permute-start.3
  9.7 1.8 copy-start.17
  11.0 0.7 copy-start.19
  13.2 1.7 collective-permute-start.4
  22.4 67.3 %reduce-scatter.8.cloned.1.call-start = ((), (), s32[]{:S(2)}) async-start(), calls=%async_computation.6 | async-start | bytes 1310720 | tf_op jit(solution)/shard_map/reduce_scatter | solution.py:108
  52.4 1.7 collective-permute-start.5
  63.7 88.2 %reduce-scatter.10.cloned.1.call-start = ((), (), s32[]{:S(2)}) async-start(), calls=%async_computation.7 | async-start | bytes 1310720 | tf_op jit(solution)/shard_map/reduce_scatter | solution.py:108
  64.0 28.6 %collective-permute-start.1 = (s32[4]{0:T(128)S(1)}, s32[4]{0:T(128)S(1)}, u32[]{:S(2)}, u32[]{:S(2)}) collective-permute-start(s32[4]{0:T(128)S(1)} %get-tuple-element.46), channel_id=1, source_target_pairs={{0,2},{2,0},{1,3},{3,1},{4,6},{6,4},{5,7},{7,5},{8,10},{10,8},{9,1... | collective-permute-start | bytes 56 | tf_op jit(solution)/shard_map/ppermute | solution.py:16
  90.7 7.7 %collective-permute-start.6 = (bf16[512,256]{0,1:T(8,128)(2,1)S(1)}, bf16[512,256]{0,1:T(8,128)(2,1)S(1)}, u32[]{:S(2)}, u32[]{:S(2)}) collective-permute-start(bf16[512,256]{0,1:T(8,128)(2,1)S(1)} %get-tuple-element.12), channel_id=1, source_target_pairs={{0,2},{2,0},{1,3},{3,1},{4,6},{6,4},{5,7},{7,5},{8,10},{10,8},{9,1... | collective-permute-start | bytes 786440 | tf_op jit(solution)/shard_map/ppermute | solution.py:16
  100.6 6.9 %collective-permute-start.7 = (bf16[1,512,256]{1,2,0:T(8,128)(2,1)S(1)}, bf16[1,512,256]{1,2,0:T(8,128)(2,1)S(1)}, u32[]{:S(2)}, u32[]{:S(2)}) collective-permute-start(bf16[1,512,256]{1,2,0:T(8,128)(2,1)S(1)} %add_convert_fusion), channel_id=1, source_target_pairs={{0,2},{2,0},{1,3},{3,1},{4,6},{6,4},{5,7},{7,5},{8,10},{10,8},{9,1... | collective-permute-start | bytes 786440 | tf_op jit(solution)/shard_map/ppermute | solution.py:16
  107.5 2.0 collective-permute-start.8
  111.4 1.5 copy-start.14
  125.3 78.6 %reduce-scatter.12.cloned.1.call-start = ((), (), s32[]{:S(2)}) async-start(), calls=%async_computation.8 | async-start | bytes 1310720 | tf_op jit(solution)/shard_map/reduce_scatter | solution.py:108
  151.9 7.9 %collective-permute-start.9 = (bf16[1,512,256]{1,2,0:T(8,128)(2,1)}, bf16[1,512,256]{1,2,0:T(8,128)(2,1)S(1)}, u32[]{:S(2)}, u32[]{:S(2)}) collective-permute-start(bf16[1,512,256]{1,2,0:T(8,128)(2,1)} %bitcast.277), channel_id=1, source_target_pairs={{0,2},{2,0},{1,3},{3,1},{4,6},{6,4},{5,7},{7,5},{8,10},{10,8},{9,1... | collective-permute-start | bytes 786440 | tf_op jit(solution)/shard_map/ppermute | solution.py:16
  160.9 2.0 collective-permute-start.10
  177.6 100.4 %reduce-scatter.14.cloned.1.call-start = ((), (), s32[]{:S(2)}) async-start(), calls=%async_computation.9 | async-start | bytes 1310720 | tf_op jit(solution)/shard_map/reduce_scatter | solution.py:108
  204.9 7.9 %collective-permute-start.11 = (bf16[512,256]{0,1:T(8,128)(2,1)S(1)}, bf16[512,256]{0,1:T(8,128)(2,1)S(1)}, u32[]{:S(2)}, u32[]{:S(2)}) collective-permute-start(bf16[512,256]{0,1:T(8,128)(2,1)S(1)} %get-tuple-element.10), channel_id=1, source_target_pairs={{0,4},{4,0},{1,5},{5,1},{2,6},{6,2},{3,7},{7,3},{8,12},{12,8},{9,1... | collective-permute-start | bytes 786440 | tf_op jit(solution)/shard_map/ppermute | solution.py:16
  206.5 6.3 %collective-permute-start = (s32[4]{0:T(128)S(1)}, s32[4]{0:T(128)S(1)}, u32[]{:S(2)}, u32[]{:S(2)}) collective-permute-start(s32[4]{0:T(128)S(1)} %get-tuple-element.44), channel_id=1, source_target_pairs={{0,4},{4,0},{1,5},{5,1},{2,6},{6,2},{3,7},{7,3},{8,12},{12,8},{9,1... | collective-permute-start | bytes 56 | tf_op jit(solution)/shard_map/ppermute | solution.py:16
  215.7 5.0 collective-permute-start.15
  217.2 6.4 %collective-permute-start.12 = (bf16[1,512,128]{2,1,0:T(8,128)(2,1)S(1)}, bf16[1,512,128]{2,1,0:T(8,128)(2,1)S(1)}, u32[]{:S(2)}, u32[]{:S(2)}) collective-permute-start(bf16[1,512,128]{2,1,0:T(8,128)(2,1)S(1)} %get-tuple-element.43), channel_id=1, source_target_pairs={{0,2},{2,0},{1,3},{3,1},{4,6},{6,4},{5,7},{7,5},{8,10},{10,8},{9,1... | collective-permute-start | bytes 393224 | tf_op jit(solution)/shard_map/ppermute | solution.py:16
  220.8 7.0 %collective-permute-start.16 = (bf16[2,512,128]{2,1,0:T(8,128)(2,1)S(1)}, bf16[2,512,128]{2,1,0:T(8,128)(2,1)S(1)}, u32[]{:S(2)}, u32[]{:S(2)}) collective-permute-start(bf16[2,512,128]{2,1,0:T(8,128)(2,1)S(1)} %maximum_select_fusion.13), channel_id=1, source_target_pairs={{0,2},{2,0},{1,3},{3,1},{4,6},{6,4},{5,7},{7,5},{8,10},{10,8},{9,1... | collective-permute-start | bytes 786440 | tf_op jit(solution)/shard_map/ppermute | solution.py:16
  223.6 6.4 %collective-permute-start.13 = (bf16[2,512,128]{2,1,0:T(8,128)(2,1)S(1)}, bf16[2,512,128]{2,1,0:T(8,128)(2,1)S(1)}, u32[]{:S(2)}, u32[]{:S(2)}) collective-permute-start(bf16[2,512,128]{2,1,0:T(8,128)(2,1)S(1)} %maximum_select_fusion.11), channel_id=1, source_target_pairs={{0,4},{4,0},{1,5},{5,1},{2,6},{6,2},{3,7},{7,3},{8,12},{12,8},{9,1... | collective-permute-start | bytes 786440 | tf_op jit(solution)/shard_map/ppermute | solution.py:16
  228.1 3.5 collective-permute-start.17
  231.1 2.1 collective-permute-start.14
  253.0 53.0 %all-gather.6.cloned.1.call-start = ((), (), s32[]{:S(2)}) async-start(), calls=%async_computation.10 | async-start | bytes 1310720 | tf_op jit(solution)/shard_map/all_gather | solution.py:114
  278.1 111.0 %all-gather.8.cloned.1.call-start = ((), (), s32[]{:S(2)}) async-start(), calls=%async_computation.11 | async-start | bytes 1310720 | tf_op jit(solution)/shard_map/all_gather | solution.py:114
  306.0 1.5 copy-start.9
  333.2 2.7 collective-permute-start.18
  338.0 8.4 %collective-permute-start.21 = (bf16[2,512,128]{1,2,0:T(8,128)(2,1)S(1)}, bf16[2,512,128]{1,2,0:T(8,128)(2,1)S(1)}, u32[]{:S(2)}, u32[]{:S(2)}) collective-permute-start(bf16[2,512,128]{1,2,0:T(8,128)(2,1)S(1)} %fusion.117), channel_id=1, source_target_pairs={{0,2},{2,0},{1,3},{3,1},{4,6},{6,4},{5,7},{7,5},{8,10},{10,8},{9,1... | collective-permute-start | bytes 786440 | tf_op jit(solution)/shard_map/ppermute | solution.py:16
  339.6 8.5 %collective-permute-start.19 = (bf16[2,512,128]{1,2,0:T(8,128)(2,1)S(1)}, bf16[2,512,128]{1,2,0:T(8,128)(2,1)S(1)}, u32[]{:S(2)}, u32[]{:S(2)}) collective-permute-start(bf16[2,512,128]{1,2,0:T(8,128)(2,1)S(1)} %fusion.116), channel_id=1, source_target_pairs={{0,4},{4,0},{1,5},{5,1},{2,6},{6,2},{3,7},{7,3},{8,12},{12,8},{9,1... | collective-permute-start | bytes 786440 | tf_op jit(solution)/shard_map/ppermute | solution.py:16
  346.6 5.0 collective-permute-start.22
  348.2 5.0 collective-permute-start.20
  353.3 6.6 %copy-start = (f32[512,128]{0,1:T(8,128)}, f32[512,128]{0,1:T(8,128)S(1)}, u32[]{:S(2)}) copy-start(f32[512,128]{0,1:T(8,128)S(1)} %bitcast_add_fusion.11) | copy-start | bytes 786436
  353.3 6.4 %collective-permute-start.23 = (bf16[512,256]{0,1:T(8,128)(2,1)S(1)}, bf16[512,256]{0,1:T(8,128)(2,1)S(1)}, u32[]{:S(2)}, u32[]{:S(2)}) collective-permute-start(bf16[512,256]{0,1:T(8,128)(2,1)S(1)} %fusion.114), channel_id=1, source_target_pairs={{0,4},{4,0},{1,5},{5,1},{2,6},{6,2},{3,7},{7,3},{8,12},{12,8},{9,1... | collective-permute-start | bytes 786440 | tf_op jit(solution)/shard_map/ppermute | solution.py:16
  362.5 80.3 %all-gather.10.cloned.1.call-start = ((), (), s32[]{:S(2)}) async-start(), calls=%async_computation.12 | async-start | bytes 1310720 | tf_op jit(solution)/shard_map/all_gather | solution.py:114
  389.1 1.5 copy-start.11
  398.8 1.5 copy-start.2
  399.8 5.0 collective-permute-start.24
  404.8 9.6 %copy-start.7 = (bf16[512,256]{0,1:T(8,128)(2,1)S(1)}, bf16[512,256]{0,1:T(8,128)(2,1)}, u32[]{:S(2)}) copy-start(bf16[512,256]{0,1:T(8,128)(2,1)} %reduce-scatter.10.cloned.1.call-done) | copy-start | bytes 786436
  406.1 8.3 %collective-permute-start.25 = (bf16[512,256]{0,1:T(8,128)(2,1)S(1)}, bf16[512,256]{0,1:T(8,128)(2,1)S(1)}, u32[]{:S(2)}, u32[]{:S(2)}) collective-permute-start(bf16[512,256]{0,1:T(8,128)(2,1)S(1)} %fusion.118), channel_id=1, source_target_pairs={{0,2},{2,0},{1,3},{3,1},{4,6},{6,4},{5,7},{7,5},{8,10},{10,8},{9,1... | collective-permute-start | bytes 786440 | tf_op jit(solution)/shard_map/ppermute | solution.py:16
  415.3 99.6 %all-gather.12.cloned.1.call-start = ((), (), s32[]{:S(2)}) async-start(), calls=%async_computation.13 | async-start | bytes 1310720 | tf_op jit(solution)/shard_map/all_gather | solution.py:114
  442.8 1.5 copy-start.10
  452.5 1.5 copy-start.3
  453.4 5.0 collective-permute-start.26
  458.5 9.7 %copy-start.4 = (bf16[512,256]{0,1:T(8,128)(2,1)S(1)}, bf16[512,256]{0,1:T(8,128)(2,1)}, u32[]{:S(2)}) copy-start(bf16[512,256]{0,1:T(8,128)(2,1)} %convert_element_type.257) | copy-start | bytes 786436
  459.8 10.1 %copy-start.18 = (s32[4]{0:T(128)S(1)}, s32[4]{0:T(128)}, u32[]{:S(2)}) copy-start(s32[4]{0:T(128)} %copy-done.17) | copy-start | bytes 52
  459.8 10.1 %copy-start.20 = (s32[4]{0:T(128)S(1)}, s32[4]{0:T(128)}, u32[]{:S(2)}) copy-start(s32[4]{0:T(128)} %copy-done.19) | copy-start | bytes 52
  459.8 8.3 %collective-permute-start.27 = (bf16[512,256]{0,1:T(8,128)(2,1)S(1)}, bf16[512,256]{0,1:T(8,128)(2,1)S(1)}, u32[]{:S(2)}, u32[]{:S(2)}) collective-permute-start(bf16[512,256]{0,1:T(8,128)(2,1)S(1)} %fusion.119), channel_id=1, source_target_pairs={{0,2},{2,0},{1,3},{3,1},{4,6},{6,4},{5,7},{7,5},{8,10},{10,8},{9,1... | collective-permute-start | bytes 786440 | tf_op jit(solution)/shard_map/ppermute | solution.py:16
  468.3 13.0 %collective-permute-start.28 = (bf16[1024,256]{0,1:T(8,128)(2,1)S(1)}, bf16[1024,256]{0,1:T(8,128)(2,1)S(1)}, u32[]{:S(2)}, u32[]{:S(2)}) collective-permute-start(bf16[1024,256]{0,1:T(8,128)(2,1)S(1)} %pad_maximum_fusion.12), channel_id=1, source_target_pairs={{0,2},{2,0},{1,3},{3,1},{4,6},{6,4},{5,7},{7,5},{8,10},{10,8},{9,1... | collective-permute-start | bytes 1572872 | tf_op jit(solution)/shard_map/ppermute | solution.py:16
  487.4 64.8 %all-gather.14.cloned.1.call-start = ((), (), s32[]{:S(2)}) async-start(), calls=%async_computation.14 | async-start | bytes 1310720 | tf_op jit(solution)/shard_map/all_gather | solution.py:114
  514.9 1.5 copy-start.12
  516.4 7.4 %copy-start.6 = (bf16[512,256]{0,1:T(8,128)(2,1)S(1)}, bf16[512,256]{0,1:T(8,128)(2,1)}, u32[]{:S(2)}) copy-start(bf16[512,256]{0,1:T(8,128)(2,1)} %reduce-scatter.6.cloned.1.call-done) | copy-start | bytes 786436
  522.2 1.6 collective-permute-start.29
  552.2 1.5 copy-start.13
  559.5 1.8 copy-start.5
  559.5 2.8 copy-start.1
  559.5 1.6 collective-permute-start.30
  562.1 2.3 collective-permute-start.31
  567.5 1.8 copy-start.16
Sparse Core Ops, SparseCore 0:
  22.5 29.8 reduce-scatter.5
  63.8 25.7 reduce-scatter.7
  125.4 26.4 reduce-scatter.9
  177.7 26.0 reduce-scatter.11
  253.1 24.9 reduce-scatter.13
  279.5 26.4 all-gather.5
  362.6 26.4 all-gather.7
  415.4 27.3 all-gather.9
  487.5 27.3 all-gather.11
  524.8 27.3 all-gather.13

commit v3 on v2

--- a/solution.py
+++ b/solution.py
@@ -143,11 +143,14 @@
     return (placed[:slice_rows] + rhs_part, placed[slice_rows:])
 
 
-def extend_down(front_rows, targets, bit_count, leaf_pos, row_pos, row_size):
+def extend_down(front_parts, targets, bit_count, leaf_pos, row_pos, row_size):
     bit_pos = bit_count - 1
-    partner_rows = partner_2(front_rows.astype(jnp.bfloat16), "leaf", bit_pos).astype(jnp.float32)
+    partner_parts = [
+        partner_2(part.astype(jnp.bfloat16), "leaf", bit_pos).astype(jnp.float32)
+        for part in front_parts
+    ]
     blocks_dev = targets.shape[0]
-    has_update = front_rows.shape[0] > blocks_dev * BLOCK
+    has_update = len(front_parts) > 1
     group_size = 1 << bit_count
     position = leaf_pos & group_size - 1
     sep_blocks = group_size * row_size * blocks_dev
@@ -155,8 +158,8 @@
     partner_slots = slot_ids(
         position ^ group_size // 2, row_pos, row_size, blocks_dev, sep_blocks, has_update
     )
-    columns = front_rows.shape[1]
-    block_pool = jnp.concatenate([front_rows, partner_rows], axis=0).reshape(-1, BLOCK * columns)
+    columns = front_parts[0].shape[1]
+    block_pool = jnp.concatenate([*front_parts, *partner_parts], axis=0).reshape(-1, BLOCK * columns)
     selector = (targets[:, None] == jnp.concatenate([own_slots, partner_slots])[None, :]).astype(
         jnp.float32
     )
@@ -199,11 +202,11 @@
     partial_value = row_folded(inv_top, y_top.astype(jnp.bfloat16))
     x_top = subgroup_sum(partial_value, leaf_bits, leaf_pos)
     solutions = [x_top]
-    front_rows = x_top
+    front_parts = [x_top]
     for level_index in (1, 2):
         bit_count = leaf_bits - level_index
         x_update = extend_down(
-            front_rows, block_map[level_index - 1], bit_count + 1, leaf_pos, row_pos, row_size
+            front_parts, block_map[level_index - 1], bit_count + 1, leaf_pos, row_pos, row_size
         )
         coupled = subgroup_sum(
             row_folded(couplings[level_index], x_update.astype(jnp.bfloat16)),
@@ -217,9 +220,9 @@
             leaf_pos,
         )
         solutions.append(x_sep)
-        front_rows = jnp.concatenate([x_sep, x_update], axis=0)
+        front_parts = [x_sep, x_update]
     leaf_solution = extend_down(
-        front_rows, block_map[2], leaf_bits - 2, leaf_pos, row_pos, row_size
+        front_parts, block_map[2], leaf_bits - 2, leaf_pos, row_pos, row_size
     )
     return (jnp.stack(solutions), leaf_solution)
 

time: 586 us -> 585 us (level)
    ppermute x32 -> x34, waiting for transfers between devices: 84.1 us -> 80.7 us  [partner_2(): return lax.ppermute(block, axis, route)]
    ppermute x32 -> x34, starting transfers between devices: 26.5 us -> 27.6 us  [partner_2(): return lax.ppermute(block, axis, route)]
  transfers between devices with their start and end apart: 42 -> 44, of which waited for: 34 -> 34; matrix products, arithmetic and copies ran while one was open for 3% -> 4% of each run, Pallas kernels for 0% -> 0%
where the time goes in v3:
time: 585 us; the launch traced here: 578 us
  waiting for transfers between devices  348 us (59%)
  matrix products  114 us (19%)
  local copies, waits for them, and re-layouts  40.2 us (7%)
  other arithmetic  31.2 us (5%)
  starting transfers between devices  29.3 us (5%)
  between operations  15.8 us (3%)
    all_gather x5, waiting for transfers between devices, row_folded(): lax.all_gather(vector_half, 'row', axis=0, tiled=True)  136 us
    reduce_scatter x5, waiting for transfers between devices, row_reduced(): lax.psum_scatter(partial_value, 'row', scatter_dimension=0, tiled=True)  130 us
    ppermute x34, waiting for transfers between devices, partner_2(): return lax.ppermute(block, axis, route)  80.7 us
    dot_general x5, matrix products, forward_apply(): lax.dot_general(panel_tile[:, :, :, 0, :], turned(vector).reshape(2, posi...  57.9 us
    dot_general x5, matrix products, transposed_apply(): lax.dot_general(panel_tile[:, :, :, 0, :], turned(vector), (((0, 1), (0,...  51.7 us
    ppermute x34, starting transfers between devices, partner_2(): return lax.ppermute(block, axis, route)  27.6 us
  transfers between devices with their start and end apart: 44, of which 34 were waited for; matrix products, arithmetic and copies ran while one was open for 4% of the time, Pallas kernels for 0%

profile of v3, /device:TPU:0, one launch (start us, length us, event | category | flops | bytes accessed | tf_op | source)
XLA Modules:
  0.0 577.8 jit_solution(7847423660793290802)
XLA Ops:
  15.6 6.7 %fusion.67 = bf16[2048,256]{0,1:T(8,128)(2,1)} fusion(bf16[2,2048,2,512]{3,2,1,0:T(2,128)(2,1)} %bitcast.316, bf16[1,2,512,256]{2,3,1,0:T(8,128)(2,1)S(1)} %copy.43, bf16[1,2,512,256]{2,3,1,0:T(8,128)(2,1)S(1)} %fusion.173), kind=kOutput, calls=%fused_computation.39 | convolution fusion | flops 2148532224 | bytes 10485760 | tf_op jit(solution)/shard_map/dot_general | solution.py:31
  22.4 30.0 %reduce-scatter.6.cloned.1.call-done = bf16[512,256]{0,1:T(8,128)(2,1)} async-done(((bf16[2048,256]{0,1:T(8,128)(2,1)}), bf16[512,256]{0,1:T(8,128)(2,1)}) %reduce-scatter.6.cloned.1.call-update) | async-done | bytes 262160 | tf_op jit(solution)/shard_map/reduce_scatter | solution.py:108
  52.4 1.7 collective-permute-done.5
  57.0 6.7 %fusion.70 = bf16[2048,256]{0,1:T(8,128)(2,1)} fusion(bf16[2,2048,2,512]{3,2,1,0:T(2,128)(2,1)} %bitcast.314, bf16[1,2,512,256]{2,3,1,0:T(8,128)(2,1)S(1)} %copy.46, bf16[1,2,512,256]{2,3,1,0:T(8,128)(2,1)S(1)} %fusion.172), kind=kOutput, calls=%fused_computation.40 | convolution fusion | flops 2148532224 | bytes 10485760 | tf_op jit(solution)/shard_map/dot_general | solution.py:31
  64.0 1.5 collective-permute-start.1
  66.1 23.6 %reduce-scatter.8.cloned.1.call-done = bf16[512,256]{0,1:T(8,128)(2,1)} async-done(((bf16[2048,256]{0,1:T(8,128)(2,1)}), bf16[512,256]{0,1:T(8,128)(2,1)}) %reduce-scatter.8.cloned.1.call-update) | async-done | bytes 262160 | tf_op jit(solution)/shard_map/reduce_scatter | solution.py:108
  90.7 1.5 collective-permute-start.6
  92.6 5.8 %collective-permute-done.6 = bf16[512,256]{0,1:T(8,128)(2,1)S(1)} collective-permute-done((bf16[512,256]{0,1:T(8,128)(2,1)S(1)}, bf16[512,256]{0,1:T(8,128)(2,1)S(1)}, u32[]{:S(2)}, u32[]{:S(2)}) %collective-permute-start.6) | collective-permute-done | bytes 262176 | tf_op jit(solution)/shard_map/ppermute | solution.py:16
  100.6 1.5 collective-permute-start.7
  102.1 5.3 collective-permute-done.7
  107.7 1.8 collective-permute-done.8
  112.8 12.4 %fusion.61 = bf16[2048,256]{0,1:T(8,128)(2,1)} fusion(bf16[2,2048,4,512]{3,2,1,0:T(4,128)(2,1)} %bitcast.312, bf16[1,4,512,256]{2,3,1,0:T(8,128)(2,1)} %copy.54, bf16[1,4,512,256]{2,3,1,0:T(8,128)(2,1)S(1)} %bitcast.293), kind=kOutput, calls=%fused_computation.37 | convolution fusion | flops 4296540160 | bytes 19922944 | tf_op jit(solution)/shard_map/dot_general | solution.py:31
  125.7 26.2 %reduce-scatter.10.cloned.1.call-done = bf16[512,256]{0,1:T(8,128)(2,1)} async-done(((bf16[2048,256]{0,1:T(8,128)(2,1)}), bf16[512,256]{0,1:T(8,128)(2,1)}) %reduce-scatter.10.cloned.1.call-update) | async-done | bytes 262160 | tf_op jit(solution)/shard_map/reduce_scatter | solution.py:108
  151.9 1.5 collective-permute-start.9
  153.4 6.4 %collective-permute-done.9 = bf16[1,512,256]{1,2,0:T(8,128)(2,1)S(1)} collective-permute-done((bf16[1,512,256]{1,2,0:T(8,128)(2,1)}, bf16[1,512,256]{1,2,0:T(8,128)(2,1)S(1)}, u32[]{:S(2)}, u32[]{:S(2)}) %collective-permute-start.9) | collective-permute-done | bytes 262176 | tf_op jit(solution)/shard_map/ppermute | solution.py:16
  165.1 12.4 %fusion.64 = bf16[2048,256]{0,1:T(8,128)(2,1)} fusion(bf16[2,2048,4,512]{3,2,1,0:T(4,128)(2,1)} %bitcast.310, bf16[1,4,512,256]{2,3,1,0:T(8,128)(2,1)} %copy.59, bf16[1,4,512,256]{2,3,1,0:T(8,128)(2,1)S(1)} %bitcast.261), kind=kOutput, calls=%fused_computation.38 | convolution fusion | flops 4296540160 | bytes 19922944 | tf_op jit(solution)/shard_map/dot_general | solution.py:31
  178.2 25.6 %reduce-scatter.12.cloned.1.call-done = bf16[512,256]{0,1:T(8,128)(2,1)} async-done(((bf16[2048,256]{0,1:T(8,128)(2,1)}), bf16[512,256]{0,1:T(8,128)(2,1)}) %reduce-scatter.12.cloned.1.call-update) | async-done | bytes 262160 | tf_op jit(solution)/shard_map/reduce_scatter | solution.py:108
  204.9 1.5 collective-permute-start.11
  207.0 5.7 collective-permute-done
  215.7 1.5 collective-permute-start.15
  218.7 2.0 collective-permute-done.15
  220.8 1.5 collective-permute-start.16
  223.9 3.9 collective-permute-done.16
  228.2 1.9 collective-permute-done.13
  233.4 19.6 %fusion.73 = bf16[2048,256]{0,1:T(8,128)(2,1)} fusion(bf16[2,2048,8,512]{3,2,1,0:T(8,128)(2,1)} %bitcast.308, bf16[1,8,512,128]{2,3,1,0:T(8,128)(2,1)S(1)} %bitcast.287, bf16[1,8,512,128]{2,3,1,0:T(8,128)(2,1)S(1)} %neg.39, bf16[1,8,512,128]{2,3,1,0:T(8,128)(2,1)S(1)} %bitcast.263), kind=kOutput, calls=%fused_computation.41 | convolution fusion | flops 8607236096 | bytes 37748736 | tf_op jit(solution)/shard_map/dot_general | solution.py:31
  253.0 25.0 %reduce-scatter.14.cloned.1.call-done = bf16[512,256]{0,1:T(8,128)(2,1)} async-done(((bf16[2048,256]{0,1:T(8,128)(2,1)}), bf16[512,256]{0,1:T(8,128)(2,1)}) %reduce-scatter.14.cloned.1.call-update) | async-done | bytes 262160 | tf_op jit(solution)/shard_map/reduce_scatter | solution.py:108
  278.3 27.7 %all-gather.6.cloned.1.call-done = bf16[2048,256]{0,1:T(8,128)(2,1)} async-done(((bf16[512,256]{0,1:T(8,128)(2,1)}), bf16[2048,256]{0,1:T(8,128)(2,1)}) %all-gather.6.cloned.1.call-update) | async-done | bytes 1048592 | tf_op jit(solution)/shard_map/all_gather | solution.py:114
  307.5 23.9 %fusion = f32[256,8,512,1]{2,0,3,1:T(8,128)} fusion(bf16[2,2048,8,512]{3,2,1,0:T(8,128)(2,1)} %bitcast.309, bf16[1,2048,256]{1,2,0:T(8,128)(2,1)S(1)} %maximum_bitcast_fusion.14, bf16[1,2048,256]{1,2,0:T(8,128)(2,1)S(1)} %bitcast.288), kind=kOutput, calls=%fused_computation | convolution fusion | flops 8594128896 | bytes 39845888 | tf_op jit(solution)/shard_map/dot_general | solution.py:40
  331.4 1.7 fusion.100
  333.2 2.6 collective-permute-done.18
  335.9 1.9 bitcast_add_fusion
  338.0 1.5 collective-permute-start.21
  339.6 1.5 collective-permute-start.19
  341.1 5.3 collective-permute-done.21
  346.5 1.5 collective-permute-start.22
  348.2 1.5 collective-permute-start.20
  349.7 1.8 collective-permute-done.22
  351.6 1.6 collective-permute-done.20
  354.6 5.2 collective-permute-done.23
  362.7 26.3 %all-gather.8.cloned.1.call-done = bf16[2048,256]{0,1:T(8,128)(2,1)} async-done(((bf16[512,256]{0,1:T(8,128)(2,1)}), bf16[2048,256]{0,1:T(8,128)(2,1)}) %all-gather.8.cloned.1.call-update) | async-done | bytes 1048592 | tf_op jit(solution)/shard_map/all_gather | solution.py:114
  390.6 8.2 %fusion.6 = f32[256,4,512,1]{2,0,3,1:T(8,128)S(1)} fusion(bf16[2,2048,4,512]{3,2,1,0:T(4,128)(2,1)} %bitcast.311, bf16[1,2048,256]{1,2,0:T(8,128)(2,1)S(1)} %maximum_bitcast_fusion.15, bf16[1,2048,256]{1,2,0:T(8,128)(2,1)S(1)} %bitcast.290), kind=kOutput, calls=%fused_computation.6 | convolution fusion | flops 4299161600 | bytes 20971520 | tf_op jit(solution)/shard_map/dot_general | solution.py:40
  400.2 1.9 copy.76
  403.2 1.6 copy.77
  406.1 1.5 collective-permute-start.25
  407.6 6.8 %collective-permute-done.25 = bf16[512,256]{0,1:T(8,128)(2,1)S(1)} collective-permute-done((bf16[512,256]{0,1:T(8,128)(2,1)S(1)}, bf16[512,256]{0,1:T(8,128)(2,1)S(1)}, u32[]{:S(2)}, u32[]{:S(2)}) %collective-permute-start.25) | collective-permute-done | bytes 262176 | tf_op jit(solution)/shard_map/ppermute | solution.py:16
  415.3 27.5 %all-gather.10.cloned.1.call-done = bf16[2048,256]{0,1:T(8,128)(2,1)} async-done(((bf16[512,256]{0,1:T(8,128)(2,1)}), bf16[2048,256]{0,1:T(8,128)(2,1)}) %all-gather.10.cloned.1.call-update) | async-done | bytes 1048592 | tf_op jit(solution)/shard_map/all_gather | solution.py:114
  444.3 8.2 %fusion.4 = f32[256,4,512,1]{2,0,3,1:T(8,128)S(1)} fusion(bf16[2,2048,4,512]{3,2,1,0:T(4,128)(2,1)} %bitcast.313, bf16[1,2048,256]{1,2,0:T(8,128)(2,1)S(1)} %maximum_bitcast_fusion.16, bf16[1,2048,256]{1,2,0:T(8,128)(2,1)S(1)} %bitcast.289), kind=kOutput, calls=%fused_computation.4 | convolution fusion | flops 4299161600 | bytes 20971520 | tf_op jit(solution)/shard_map/dot_general | solution.py:40
  453.9 1.9 copy.80
  456.9 1.6 copy.81
  459.8 1.5 collective-permute-start.27
  462.0 7.1 %collective-permute-done.27 = bf16[512,256]{0,1:T(8,128)(2,1)S(1)} collective-permute-done((bf16[512,256]{0,1:T(8,128)(2,1)S(1)}, bf16[512,256]{0,1:T(8,128)(2,1)S(1)}, u32[]{:S(2)}, u32[]{:S(2)}) %collective-permute-start.27) | collective-permute-done | bytes 262176 | tf_op jit(solution)/shard_map/ppermute | solution.py:16
  469.1 1.5 collective-permute-start.28
  470.8 3.9 collective-permute-done.29
  474.7 4.6 collective-permute-done.28
  479.6 1.8 copy.84
  481.4 1.7 reshape.845
  485.6 27.2 %all-gather.12.cloned.1.call-done = bf16[2048,256]{0,1:T(8,128)(2,1)} async-done(((bf16[512,256]{0,1:T(8,128)(2,1)}), bf16[2048,256]{0,1:T(8,128)(2,1)}) %all-gather.12.cloned.1.call-update) | async-done | bytes 1048592 | tf_op jit(solution)/shard_map/all_gather | solution.py:114
  514.4 5.7 fusion.94
  520.2 1.5 collective-permute-done.30
  522.6 27.5 %all-gather.14.cloned.1.call-done = bf16[2048,256]{0,1:T(8,128)(2,1)} async-done(((bf16[512,256]{0,1:T(8,128)(2,1)}), bf16[2048,256]{0,1:T(8,128)(2,1)}) %all-gather.14.cloned.1.call-update) | async-done | bytes 1048592 | tf_op jit(solution)/shard_map/all_gather | solution.py:114
  551.7 5.7 fusion.97
  561.1 1.6 copy.90
  564.9 1.8 copy.89
  566.7 1.7 reshape.847
  (246 shorter events, 69.9 us)
Async XLA Ops:
  7.2 45.3 %reduce-scatter.6.cloned.1.call-start = ((), (), s32[]{:S(2)}) async-start(), calls=%async_computation.5 | async-start | bytes 1310720 | tf_op jit(solution)/shard_map/reduce_scatter | solution.py:108
  8.0 3.4 copy-start.15
  8.0 3.3 collective-permute-start.2
  9.6 1.9 copy-start.6
  9.6 1.8 collective-permute-start.3
  9.7 1.8 copy-start.17
  13.2 1.7 collective-permute-start.4
  22.4 67.3 %reduce-scatter.8.cloned.1.call-start = ((), (), s32[]{:S(2)}) async-start(), calls=%async_computation.6 | async-start | bytes 1310720 | tf_op jit(solution)/shard_map/reduce_scatter | solution.py:108
  52.4 1.7 collective-permute-start.5
  63.7 88.2 %reduce-scatter.10.cloned.1.call-start = ((), (), s32[]{:S(2)}) async-start(), calls=%async_computation.7 | async-start | bytes 1310720 | tf_op jit(solution)/shard_map/reduce_scatter | solution.py:108
  64.0 28.6 %collective-permute-start.1 = (s32[4]{0:T(128)S(1)}, s32[4]{0:T(128)S(1)}, u32[]{:S(2)}, u32[]{:S(2)}) collective-permute-start(s32[4]{0:T(128)S(1)} %get-tuple-element.46), channel_id=1, source_target_pairs={{0,2},{2,0},{1,3},{3,1},{4,6},{6,4},{5,7},{7,5},{8,10},{10,8},{9,1... | collective-permute-start | bytes 56 | tf_op jit(solution)/shard_map/ppermute | solution.py:16
  90.7 7.7 %collective-permute-start.6 = (bf16[512,256]{0,1:T(8,128)(2,1)S(1)}, bf16[512,256]{0,1:T(8,128)(2,1)S(1)}, u32[]{:S(2)}, u32[]{:S(2)}) collective-permute-start(bf16[512,256]{0,1:T(8,128)(2,1)S(1)} %get-tuple-element.12), channel_id=1, source_target_pairs={{0,2},{2,0},{1,3},{3,1},{4,6},{6,4},{5,7},{7,5},{8,10},{10,8},{9,1... | collective-permute-start | bytes 786440 | tf_op jit(solution)/shard_map/ppermute | solution.py:16
  100.6 6.9 %collective-permute-start.7 = (bf16[1,512,256]{1,2,0:T(8,128)(2,1)S(1)}, bf16[1,512,256]{1,2,0:T(8,128)(2,1)S(1)}, u32[]{:S(2)}, u32[]{:S(2)}) collective-permute-start(bf16[1,512,256]{1,2,0:T(8,128)(2,1)S(1)} %add_convert_fusion), channel_id=1, source_target_pairs={{0,2},{2,0},{1,3},{3,1},{4,6},{6,4},{5,7},{7,5},{8,10},{10,8},{9,1... | collective-permute-start | bytes 786440 | tf_op jit(solution)/shard_map/ppermute | solution.py:16
  107.5 2.0 collective-permute-start.8
  111.4 1.5 copy-start.14
  125.3 78.6 %reduce-scatter.12.cloned.1.call-start = ((), (), s32[]{:S(2)}) async-start(), calls=%async_computation.8 | async-start | bytes 1310720 | tf_op jit(solution)/shard_map/reduce_scatter | solution.py:108
  151.9 7.9 %collective-permute-start.9 = (bf16[1,512,256]{1,2,0:T(8,128)(2,1)}, bf16[1,512,256]{1,2,0:T(8,128)(2,1)S(1)}, u32[]{:S(2)}, u32[]{:S(2)}) collective-permute-start(bf16[1,512,256]{1,2,0:T(8,128)(2,1)} %bitcast.277), channel_id=1, source_target_pairs={{0,2},{2,0},{1,3},{3,1},{4,6},{6,4},{5,7},{7,5},{8,10},{10,8},{9,1... | collective-permute-start | bytes 786440 | tf_op jit(solution)/shard_map/ppermute | solution.py:16
  160.9 2.0 collective-permute-start.10
  177.6 100.4 %reduce-scatter.14.cloned.1.call-start = ((), (), s32[]{:S(2)}) async-start(), calls=%async_computation.9 | async-start | bytes 1310720 | tf_op jit(solution)/shard_map/reduce_scatter | solution.py:108
  204.9 7.9 %collective-permute-start.11 = (bf16[512,256]{0,1:T(8,128)(2,1)S(1)}, bf16[512,256]{0,1:T(8,128)(2,1)S(1)}, u32[]{:S(2)}, u32[]{:S(2)}) collective-permute-start(bf16[512,256]{0,1:T(8,128)(2,1)S(1)} %get-tuple-element.10), channel_id=1, source_target_pairs={{0,4},{4,0},{1,5},{5,1},{2,6},{6,2},{3,7},{7,3},{8,12},{12,8},{9,1... | collective-permute-start | bytes 786440 | tf_op jit(solution)/shard_map/ppermute | solution.py:16
  206.5 6.3 %collective-permute-start = (s32[4]{0:T(128)S(1)}, s32[4]{0:T(128)S(1)}, u32[]{:S(2)}, u32[]{:S(2)}) collective-permute-start(s32[4]{0:T(128)S(1)} %get-tuple-element.44), channel_id=1, source_target_pairs={{0,4},{4,0},{1,5},{5,1},{2,6},{6,2},{3,7},{7,3},{8,12},{12,8},{9,1... | collective-permute-start | bytes 56 | tf_op jit(solution)/shard_map/ppermute | solution.py:16
  215.7 5.0 collective-permute-start.15
  217.2 6.4 %collective-permute-start.12 = (bf16[1,512,128]{2,1,0:T(8,128)(2,1)S(1)}, bf16[1,512,128]{2,1,0:T(8,128)(2,1)S(1)}, u32[]{:S(2)}, u32[]{:S(2)}) collective-permute-start(bf16[1,512,128]{2,1,0:T(8,128)(2,1)S(1)} %get-tuple-element.43), channel_id=1, source_target_pairs={{0,2},{2,0},{1,3},{3,1},{4,6},{6,4},{5,7},{7,5},{8,10},{10,8},{9,1... | collective-permute-start | bytes 393224 | tf_op jit(solution)/shard_map/ppermute | solution.py:16
  220.8 7.0 %collective-permute-start.16 = (bf16[2,512,128]{2,1,0:T(8,128)(2,1)S(1)}, bf16[2,512,128]{2,1,0:T(8,128)(2,1)S(1)}, u32[]{:S(2)}, u32[]{:S(2)}) collective-permute-start(bf16[2,512,128]{2,1,0:T(8,128)(2,1)S(1)} %maximum_select_fusion.13), channel_id=1, source_target_pairs={{0,2},{2,0},{1,3},{3,1},{4,6},{6,4},{5,7},{7,5},{8,10},{10,8},{9,1... | collective-permute-start | bytes 786440 | tf_op jit(solution)/shard_map/ppermute | solution.py:16
  223.6 6.4 %collective-permute-start.13 = (bf16[2,512,128]{2,1,0:T(8,128)(2,1)S(1)}, bf16[2,512,128]{2,1,0:T(8,128)(2,1)S(1)}, u32[]{:S(2)}, u32[]{:S(2)}) collective-permute-start(bf16[2,512,128]{2,1,0:T(8,128)(2,1)S(1)} %maximum_select_fusion.11), channel_id=1, source_target_pairs={{0,4},{4,0},{1,5},{5,1},{2,6},{6,2},{3,7},{7,3},{8,12},{12,8},{9,1... | collective-permute-start | bytes 786440 | tf_op jit(solution)/shard_map/ppermute | solution.py:16
  228.1 3.5 collective-permute-start.17
  231.2 2.1 collective-permute-start.14
  253.0 53.0 %all-gather.6.cloned.1.call-start = ((), (), s32[]{:S(2)}) async-start(), calls=%async_computation.10 | async-start | bytes 1310720 | tf_op jit(solution)/shard_map/all_gather | solution.py:114
  278.1 111.0 %all-gather.8.cloned.1.call-start = ((), (), s32[]{:S(2)}) async-start(), calls=%async_computation.11 | async-start | bytes 1310720 | tf_op jit(solution)/shard_map/all_gather | solution.py:114
  306.0 1.5 copy-start.9
  333.1 2.7 collective-permute-start.18
  338.0 8.4 %collective-permute-start.21 = (bf16[2,512,128]{1,2,0:T(8,128)(2,1)S(1)}, bf16[2,512,128]{1,2,0:T(8,128)(2,1)S(1)}, u32[]{:S(2)}, u32[]{:S(2)}) collective-permute-start(bf16[2,512,128]{1,2,0:T(8,128)(2,1)S(1)} %fusion.117), channel_id=1, source_target_pairs={{0,2},{2,0},{1,3},{3,1},{4,6},{6,4},{5,7},{7,5},{8,10},{10,8},{9,1... | collective-permute-start | bytes 786440 | tf_op jit(solution)/shard_map/ppermute | solution.py:16
  339.6 8.5 %collective-permute-start.19 = (bf16[2,512,128]{1,2,0:T(8,128)(2,1)S(1)}, bf16[2,512,128]{1,2,0:T(8,128)(2,1)S(1)}, u32[]{:S(2)}, u32[]{:S(2)}) collective-permute-start(bf16[2,512,128]{1,2,0:T(8,128)(2,1)S(1)} %fusion.116), channel_id=1, source_target_pairs={{0,4},{4,0},{1,5},{5,1},{2,6},{6,2},{3,7},{7,3},{8,12},{12,8},{9,1... | collective-permute-start | bytes 786440 | tf_op jit(solution)/shard_map/ppermute | solution.py:16
  346.5 5.0 collective-permute-start.22
  348.2 5.0 collective-permute-start.20
  353.3 6.6 %copy-start = (f32[512,128]{0,1:T(8,128)}, f32[512,128]{0,1:T(8,128)S(1)}, u32[]{:S(2)}) copy-start(f32[512,128]{0,1:T(8,128)S(1)} %bitcast_add_fusion.11) | copy-start | bytes 786436
  353.3 6.4 %collective-permute-start.23 = (bf16[512,256]{0,1:T(8,128)(2,1)S(1)}, bf16[512,256]{0,1:T(8,128)(2,1)S(1)}, u32[]{:S(2)}, u32[]{:S(2)}) collective-permute-start(bf16[512,256]{0,1:T(8,128)(2,1)S(1)} %fusion.114), channel_id=1, source_target_pairs={{0,4},{4,0},{1,5},{5,1},{2,6},{6,2},{3,7},{7,3},{8,12},{12,8},{9,1... | collective-permute-start | bytes 786440 | tf_op jit(solution)/shard_map/ppermute | solution.py:16
  362.4 80.3 %all-gather.10.cloned.1.call-start = ((), (), s32[]{:S(2)}) async-start(), calls=%async_computation.12 | async-start | bytes 1310720 | tf_op jit(solution)/shard_map/all_gather | solution.py:114
  389.0 1.5 copy-start.11
  398.7 1.5 copy-start.2
  399.7 5.0 collective-permute-start.24
  404.7 9.6 %copy-start.5 = (bf16[512,256]{0,1:T(8,128)(2,1)S(1)}, bf16[512,256]{0,1:T(8,128)(2,1)}, u32[]{:S(2)}) copy-start(bf16[512,256]{0,1:T(8,128)(2,1)} %reduce-scatter.10.cloned.1.call-done) | copy-start | bytes 786436
  406.1 8.3 %collective-permute-start.25 = (bf16[512,256]{0,1:T(8,128)(2,1)S(1)}, bf16[512,256]{0,1:T(8,128)(2,1)S(1)}, u32[]{:S(2)}, u32[]{:S(2)}) collective-permute-start(bf16[512,256]{0,1:T(8,128)(2,1)S(1)} %fusion.118), channel_id=1, source_target_pairs={{0,2},{2,0},{1,3},{3,1},{4,6},{6,4},{5,7},{7,5},{8,10},{10,8},{9,1... | collective-permute-start | bytes 786440 | tf_op jit(solution)/shard_map/ppermute | solution.py:16
  415.2 97.6 %all-gather.12.cloned.1.call-start = ((), (), s32[]{:S(2)}) async-start(), calls=%async_computation.13 | async-start | bytes 1310720 | tf_op jit(solution)/shard_map/all_gather | solution.py:114
  442.7 1.5 copy-start.10
  452.5 1.5 copy-start.3
  453.4 5.1 collective-permute-start.26
  458.4 2.9 copy-start.7
  458.5 12.2 %copy-start.18 = (s32[4]{0:T(128)S(1)}, s32[4]{0:T(128)}, u32[]{:S(2)}) copy-start(s32[4]{0:T(128)} %copy-done.17) | copy-start | bytes 52
  458.5 12.2 %copy-start.20 = (s32[4]{0:T(128)S(1)}, s32[4]{0:T(128)}, u32[]{:S(2)}) copy-start(s32[4]{0:T(128)} %copy-done.19) | copy-start | bytes 52
  459.8 9.2 %collective-permute-start.27 = (bf16[512,256]{0,1:T(8,128)(2,1)S(1)}, bf16[512,256]{0,1:T(8,128)(2,1)S(1)}, u32[]{:S(2)}, u32[]{:S(2)}) collective-permute-start(bf16[512,256]{0,1:T(8,128)(2,1)S(1)} %fusion.119), channel_id=1, source_target_pairs={{0,2},{2,0},{1,3},{3,1},{4,6},{6,4},{5,7},{7,5},{8,10},{10,8},{9,1... | collective-permute-start | bytes 786440 | tf_op jit(solution)/shard_map/ppermute | solution.py:16
  461.3 13.3 %collective-permute-start.29 = (bf16[512,256]{0,1:T(8,128)(2,1)S(1)}, bf16[512,256]{0,1:T(8,128)(2,1)S(1)}, u32[]{:S(2)}, u32[]{:S(2)}) collective-permute-start(bf16[512,256]{0,1:T(8,128)(2,1)S(1)} %copy-done.7), channel_id=1, source_target_pairs={{0,2},{2,0},{1,3},{3,1},{4,6},{6,4},{5,7},{7,5},{8,10},{10,8},{9,1... | collective-permute-start | bytes 786440 | tf_op jit(solution)/shard_map/ppermute | solution.py:16
  469.1 10.2 %collective-permute-start.28 = (bf16[512,256]{0,1:T(8,128)(2,1)S(1)}, bf16[512,256]{0,1:T(8,128)(2,1)S(1)}, u32[]{:S(2)}, u32[]{:S(2)}) collective-permute-start(bf16[512,256]{0,1:T(8,128)(2,1)S(1)} %get-tuple-element.8), channel_id=1, source_target_pairs={{0,2},{2,0},{1,3},{3,1},{4,6},{6,4},{5,7},{7,5},{8,10},{10,8},{9,1... | collective-permute-start | bytes 786440 | tf_op jit(solution)/shard_map/ppermute | solution.py:16
  485.3 64.8 %all-gather.14.cloned.1.call-start = ((), (), s32[]{:S(2)}) async-start(), calls=%async_computation.14 | async-start | bytes 1310720 | tf_op jit(solution)/shard_map/all_gather | solution.py:114
  512.8 1.5 copy-start.12
  514.4 7.4 %copy-start.4 = (bf16[512,256]{0,1:T(8,128)(2,1)S(1)}, bf16[512,256]{0,1:T(8,128)(2,1)}, u32[]{:S(2)}) copy-start(bf16[512,256]{0,1:T(8,128)(2,1)} %reduce-scatter.6.cloned.1.call-done) | copy-start | bytes 786436
  520.2 1.6 collective-permute-start.30
  550.1 1.5 copy-start.13
  551.7 5.9 %copy-start.8 = (bf16[512,256]{0,1:T(8,128)(2,1)S(1)}, bf16[512,256]{0,1:T(8,128)(2,1)}, u32[]{:S(2)}) copy-start(bf16[512,256]{0,1:T(8,128)(2,1)} %convert_element_type.287) | copy-start | bytes 786436
  557.4 2.6 copy-start.1
  557.5 1.6 collective-permute-start.31
  557.6 2.5 collective-permute-start.33
  559.9 2.8 collective-permute-start.32
  566.7 1.8 copy-start.16
  (1 other events, 0.7 us)
Sparse Core Ops, SparseCore 0:
  22.5 29.8 reduce-scatter.5
  63.8 25.7 reduce-scatter.7
  125.4 26.4 reduce-scatter.9
  177.7 26.0 reduce-scatter.11
  253.1 24.8 reduce-scatter.13
  279.5 26.4 all-gather.5
  362.6 26.4 all-gather.7
  415.3 27.3 all-gather.9
  485.4 27.3 all-gather.11
  522.7 27.3 all-gather.13
